TPU v7x, 768 devices: a whole 4x8x12 slice. The times are simulated.
768 devices in a mesh: stream: 24 (over x, z_lo, core), girth: 32 (over z_hi, y).
Axes of the slice: x: 4, y: 8, z: 12 (z_hi: 4, z_lo: 3; z = z_hi * 3 + z_lo), core: 2. Of those that a mesh axis runs over, the one named last changes fastest.
Arguments:
- velocity: float32 [3, 768, 512, 128], P(None, 'stream', 'girth'), may hold values from -6 to 6
- pressure: float32 [768, 512, 128], P('stream', 'girth'), may hold values from -6 to 6
- turb_k: float32 [768, 512, 128], P('stream', 'girth'), may hold values from 0.05 to 0.5
- turb_omega: float32 [768, 512, 128], P('stream', 'girth'), may hold values from 0.5 to 5
- face_code: int32 [24, 32, 2], P('stream', 'girth'), may hold values from 0 to 1, as said below
- disc_cells: int32 [24, 16384], P('stream', 'girth'), may hold values from 0 to 65535
- disc_sector: int32 [24, 16384, 1], P('stream', 'girth'), may hold values from 0 to 31, as said below
- disc_weight: float32 [24, 16384], P('stream', 'girth'), may hold values from 0.2 to 2
Outputs:
- velocity_out: float32 [3, 768, 512, 128], P(None, 'stream', 'girth')
- pressure_out: float32 [768, 512, 128], P('stream', 'girth')
Inputs may be any that keep to these rules, and one draw needn't show every extreme that they name: face_code[s, g, 1] equals face_code[s, (g + 1) mod 32, 0]. `disc_sector`: the 512 disc cells of one block name any one sector at most 32 times, and every block names some sector exactly 32 times. In some rows of blocks a sector is named by no block of the row.
All inputs are finite; a program needn't handle non-finite values.
Results may differ from a plain program's by a relative error of at most 0.000073.
Values sent between devices are 32-bit elements; how exact they have to be, the bound alone decides.
No kernel may reach another device: no remote copies, remote signals or barrier semaphores. Data moves between devices by JAX's collectives and lax.ppermute only.
A program may use at most 64 MiB of HBM per device.

v0:
```python
import jax
import jax.numpy as jnp
from jax import lax
from jax.sharding import PartitionSpec as P

time_step = 0.5
viscosity = 0.02
advect = 0.25
thrust = 8.0
target_speed = 0.5


def extended(value, sides, width):
    for axis, dim in sides:
        peers, length = (lax.axis_size(axis), value.shape[dim])
        up = [(i, (i + 1) % peers) for i in range(peers)]
        down = [(j, i) for i, j in up]
        last = lax.slice_in_dim(value, length - width, length, axis=dim)
        initial = lax.slice_in_dim(value, 0, width, axis=dim)
        before = lax.ppermute(last, axis, up)
        after = lax.ppermute(initial, axis, down)
        value = jnp.concatenate([before, value, after], axis=dim)
    return value


def edge_values(values):
    return jnp.array(values, jnp.float32).reshape(-1, 1, 1, 1)


def stream_pair(padded, inlet_value, outlet_value):
    centre = padded[:, 1:-1]
    at_inlet = lax.axis_index("stream") == 0
    at_outlet = lax.axis_index("stream") == lax.axis_size("stream") - 1
    low_side = padded[:, :-2]
    high_side = padded[:, 2:]
    low_side = jnp.concatenate(
        [jnp.where(at_inlet, inlet_value * centre[:, :1], low_side[:, :1]), low_side[:, 1:]], axis=1
    )
    high_side = jnp.concatenate(
        [high_side[:, :-1], jnp.where(at_outlet, outlet_value * centre[:, -1:], high_side[:, -1:])],
        axis=1,
    )
    return (low_side, high_side)


def girth_pair(padded, orient):
    low_side = padded[:, :, :-2]
    high_side = padded[:, :, 2:]
    low_edge = low_side[:, :, :1]
    high_edge = high_side[:, :, -1:]
    low_edge = jnp.where(orient[0] == 1, low_edge[..., ::-1], low_edge)
    high_edge = jnp.where(orient[1] == 1, high_edge[..., ::-1], high_edge)
    low_side = jnp.concatenate([low_edge, low_side[:, :, 1:]], axis=2)
    high_side = jnp.concatenate([high_side[:, :, :-1], high_edge], axis=2)
    return (low_side, high_side)


def normal_pair(centre, wall_sign):
    low_side = jnp.concatenate([wall_sign * centre[..., :1], centre[..., :-1]], axis=3)
    high_side = jnp.concatenate([centre[..., 1:], jnp.zeros_like(centre[..., :1])], axis=3)
    return (low_side, high_side)


def surround(fields, inlet_value, outlet_value, wall_sign, orient):
    padded = extended(fields, (("stream", 1), ("girth", 2)), 1)
    return (
        stream_pair(padded[:, :, 1:-1], inlet_value, outlet_value),
        girth_pair(padded[:, 1:-1], orient),
        normal_pair(fields, wall_sign),
    )


def spread(sides):
    return sides[0][0] + sides[0][1] + sides[1][0] + sides[1][1] + sides[2][0] + sides[2][1]


def body(velocity, pressure, turb_k, turb_omega, face_code, disc_cells, disc_sector, disc_weight):
    orient = face_code[0, 0]
    girth_count = lax.axis_size("girth")
    cell_list = disc_cells[0]
    owners = disc_sector[0, :, 0]
    disc_rows = cell_list.shape[0]
    inflow = velocity[0].reshape(-1)[cell_list]
    sector_hot = (owners[:, None] == jnp.arange(girth_count, dtype=jnp.int32)[None, :]).astype(
        jnp.float32
    )
    capacity = 2 * disc_rows // girth_count
    position = jnp.arange(disc_rows, dtype=jnp.int32)
    earlier = (position[:, None] > position[None, :]) & (owners[:, None] == owners[None, :])
    slot_rank = jnp.sum(earlier.astype(jnp.int32), axis=1)
    slot_hot = (slot_rank[:, None] == jnp.arange(capacity, dtype=jnp.int32)[None, :]).astype(
        jnp.float32
    )
    send_values = jnp.dot(
        (sector_hot * inflow[:, None]).T, slot_hot, precision=lax.Precision.HIGHEST
    )
    send_marks = jnp.dot(sector_hot.T, slot_hot, precision=lax.Precision.HIGHEST)
    got_values, got_marks = (
        lax.all_to_all(send_values, "girth", split_axis=0, concat_axis=0, tiled=True),
        lax.all_to_all(send_marks, "girth", split_axis=0, concat_axis=0, tiled=True),
    )
    own_average = jnp.sum(got_values) / jnp.maximum(jnp.sum(got_marks), 1.0)
    own_load = (thrust * (target_speed - own_average)).reshape(1)
    sector_load = lax.all_gather(own_load, "girth", axis=0, tiled=True)
    cell_load = jnp.dot(sector_hot, sector_load, precision=lax.Precision.HIGHEST) * disc_weight[0]
    forcing = (
        jnp.zeros((velocity[0].size,), jnp.float32)
        .at[cell_list]
        .add(cell_load)
        .reshape(velocity.shape[1:])
    )
    effective = viscosity + turb_k / turb_omega
    speed_in = edge_values([0.0, 0.0, 0.0])
    speed_out = edge_values([1.0, 1.0, 1.0])
    speed_wall = edge_values([-1.0, -1.0, -1.0])
    press_in = edge_values([1.0])
    press_out = edge_values([0.0])
    press_wall = edge_values([1.0])
    moving_in = edge_values([0.0, 0.0, 0.0, 1.0])
    moving_out = edge_values([1.0, 1.0, 1.0, 0.0])
    moving_wall = edge_values([-1.0, -1.0, -1.0, 1.0])
    moving = jnp.concatenate([velocity, pressure[None]], axis=0)
    both_sides = surround(moving, moving_in, moving_out, moving_wall, orient)
    sides = tuple(((pair[0][:3], pair[1][:3]) for pair in both_sides))
    press_sides = tuple(((pair[0][3:], pair[1][3:]) for pair in both_sides))
    gradient = jnp.concatenate(
        [
            press_sides[0][1] - press_sides[0][0],
            press_sides[1][1] - press_sides[1][0],
            press_sides[2][1] - press_sides[2][0],
        ],
        axis=0,
    )
    push = jnp.concatenate([forcing[None], jnp.zeros_like(velocity[1:])], axis=0)
    u_star = (
        velocity
        - time_step * advect * (sides[0][1] - sides[0][0])
        + time_step * effective * spread(sides)
        - 0.5 * time_step * gradient
        + time_step * push
    ) / (1.0 + 6.0 * time_step * effective)
    star_sides = surround(u_star, speed_in, speed_out, speed_wall, orient)
    outflow = 0.5 * (
        star_sides[0][1][0]
        - star_sides[0][0][0]
        + (star_sides[1][1][1] - star_sides[1][0][1])
        + (star_sides[2][1][2] - star_sides[2][0][2])
    )
    first_sweep = -outflow / (6.0 * time_step)
    first_sides = surround(first_sweep[None], press_in, press_out, press_wall, orient)
    second_sweep = (spread(first_sides)[0] - outflow / time_step) / 6.0
    second_sides = surround(second_sweep[None], press_in, press_out, press_wall, orient)
    correction = jnp.concatenate(
        [
            second_sides[0][1] - second_sides[0][0],
            second_sides[1][1] - second_sides[1][0],
            second_sides[2][1] - second_sides[2][0],
        ],
        axis=0,
    )
    velocity_out = u_star - 0.5 * time_step * correction
    pressure_out = pressure + second_sweep
    return (velocity_out, pressure_out)


def solution(mesh):
    placed = (
        P(None, "stream", "girth", None),
        P("stream", "girth", None),
        P("stream", "girth", None),
        P("stream", "girth", None),
        P("stream", "girth", None),
        P("stream", "girth"),
        P("stream", "girth", None),
        P("stream", "girth"),
    )
    return jax.shard_map(
        body,
        mesh=mesh,
        in_specs=placed,
        out_specs=(P(None, "stream", "girth", None), P("stream", "girth", None)),
        check_vma=False,
    )
```

profile of v0, /device:TPU:248, one launch (start us, length us, event | category | flops | bytes accessed | tf_op | source)
XLA Modules:
  0.0 272.5 jit_solution(12969781047565425465)
XLA Ops:
  0.6 1.0 convert_reduce_fusion
  1.7 1.0 fusion.37
  2.7 17.0 %all-to-all-start.1 = ((f32[32,1,32]{2,1,0:T(1,128)}), f32[32,1,32]{2,1,0:T(1,128)S(1)}, u32[]{:S(2)}, u32[]{:S(2)}) async-start(f32[32,1,32]{2,1,0:T(1,128)} %bitcast.10), calls=%async_computation.1 | async-start | bytes 32768 | tf_op jit(solution)/shard_map/all_to_all | solution.py:100
  19.6 0.8 fusion.51
  20.5 6.1 %collective-permute-start = (f32[4,1,16,128]{3,2,1,0:T(8,128)S(1)}, f32[4,1,16,128]{3,2,1,0:T(8,128)S(1)}, u32[]{:S(2)}, u32[]{:S(2)}) collective-permute-start(f32[4,1,16,128]{3,2,1,0:T(8,128)S(1)} %fusion.51), channel_id=1, source_target_pairs={{32,0},{64,32},{96,64},{128,96},{160,128},{192,160},{224,192},{256... | collective-permute-start | bytes 98312 | tf_op jit(solution)/shard_map/ppermute | solution.py:21
  26.6 1.3 select_maximum_fusion
  27.9 1.0 fusion
  29.0 1.2 fusion.1
  30.2 3.1 %gather_fusion = f32[512]{0:T(512)S(1)} fusion(f32[65536]{0:T(1024)S(1)} %bitcast.26, s32[1024]{0:T(1024)S(1)} %pad_clamp_fusion), kind=kCustom, calls=%fused_computation | custom fusion | bytes 6144 | tf_op jit(solution)/shard_map/gather | solution.py:83
  33.3 1.2 fusion.38
  34.8 0.8 copy-done.9
  35.6 0.9 broadcast_multiply_fusion
  36.5 0.3 copy-done.5
  36.8 0.6 copy-done.3
  37.4 1.1 fusion.28
  38.5 1.5 fusion.6
  40.0 14.7 %all-to-all-start = ((f32[32,1,32]{2,1,0:T(1,128)}), f32[32,1,32]{2,1,0:T(1,128)S(1)}, u32[]{:S(2)}, u32[]{:S(2)}) async-start(f32[32,1,32]{2,1,0:T(1,128)} %bitcast.8), calls=%async_computation | async-start | bytes 32768 | tf_op jit(solution)/shard_map/all_to_all | solution.py:99
  54.7 0.6 fusion.69
  56.5 1.3 dynamic-slice
  57.8 0.7 reduce_sum.29
  59.2 4.9 %all-to-all-done = f32[32,1,32]{2,1,0:T(1,128)S(1)} async-done(((f32[32,1,32]{2,1,0:T(1,128)}), f32[32,1,32]{2,1,0:T(1,128)S(1)}, u32[]{:S(2)}, u32[]{:S(2)}) %all-to-all-start) | async-done | bytes 4128 | tf_op jit(solution)/shard_map/all_to_all | solution.py:99
  64.1 0.6 reduce_sum.28
  65.4 0.7 dynamic-update-slice
  66.2 83.8 %all-reduce.5 = f32[32]{0:T(128)S(1)} all-reduce(f32[32]{0:T(128)S(1)} %dynamic-update-slice), channel_id=1, replica_groups=mesh['stream'=24,'girth'=32] {'girth'}, use_global_device_ids=true, to_apply=%add.5 | all-reduce | flops 32 | bytes 256
  150.0 1.9 collective-permute-start.1
  151.9 0.3 fusion.40
  152.2 0.7 copy-done.12
  152.9 3.9 %scatter_custom_fusion = f32[65536]{0:T(1024)} fusion(s32[512]{0:T(512)S(1)} %bitcast.39, f32[512]{0:T(512)S(1)} %mul.158, f32[]{:T(128)} %constant.65.clone), kind=kCustom, calls=%fused_computation.104 | custom fusion | flops 512 | bytes 262148 | tf_op jit(solution)/shard_map/scatter-add | solution.py:109
  156.9 2.6 collective-permute-done.1
  159.6 9.3 %collective-permute-start.2 = (f32[4,34,1,128]{3,2,1,0:T(1,128)S(1)}, f32[4,34,1,128]{3,2,1,0:T(1,128)S(1)}, u32[]{:S(2)}, u32[]{:S(2)}) collective-permute-start(f32[4,34,1,128]{3,2,1,0:T(1,128)S(1)} %get-tuple-element.8), channel_id=1, source_target_pairs={{0,1},{1,2},{2,3},{3,4},{4,5},{5,6},{6,7},{7,8},{8,9},{9,10},{10,1... | collective-permute-start | bytes 208904 | tf_op jit(solution)/shard_map/ppermute | solution.py:20
  168.9 1.9 collective-permute-start.3
  170.9 1.1 fusion.30
  172.0 0.3 rev.24
  172.3 8.0 %collective-permute-done.3 = f32[4,34,1,128]{3,2,1,0:T(1,128)S(1)} collective-permute-done((f32[4,34,1,128]{3,2,1,0:T(1,128)S(1)}, f32[4,34,1,128]{3,2,1,0:T(1,128)S(1)}, u32[]{:S(2)}, u32[]{:S(2)}) %collective-permute-start.3) | collective-permute-done | bytes 69664 | tf_op jit(solution)/shard_map/ppermute | solution.py:21
  180.3 0.3 rev.25
  180.8 1.2 fusion.29
  182.1 0.3 copy-done.4
  182.4 2.5 fusion.15
  184.9 1.3 fusion.57
  186.2 1.1 fusion.60
  187.3 1.3 fusion.58
  188.6 1.9 collective-permute-start.5
  190.5 7.9 %collective-permute-start.4 = (f32[3,1,16,128]{3,2,1,0:T(8,128)S(1)}, f32[3,1,16,128]{3,2,1,0:T(8,128)S(1)}, u32[]{:S(2)}, u32[]{:S(2)}) collective-permute-start(f32[3,1,16,128]{3,2,1,0:T(8,128)S(1)} %get-tuple-element.23), channel_id=1, source_target_pairs={{32,0},{64,32},{96,64},{128,96},{160,128},{192,160},{224,192},{256... | collective-permute-start | bytes 73736 | tf_op jit(solution)/shard_map/ppermute | solution.py:21
  198.5 1.4 collective-permute-done.4
  200.0 1.9 collective-permute-start.6
  201.9 9.0 %collective-permute-start.7 = (f32[3,34,1,128]{3,2,1,0:T(1,128)S(1)}, f32[3,34,1,128]{3,2,1,0:T(1,128)S(1)}, u32[]{:S(2)}, u32[]{:S(2)}) collective-permute-start(f32[3,34,1,128]{3,2,1,0:T(1,128)S(1)} %get-tuple-element.15), channel_id=1, source_target_pairs={{0,1},{1,2},{2,3},{3,4},{4,5},{5,6},{6,7},{7,8},{8,9},{9,10},{10,1... | collective-permute-start | bytes 156680 | tf_op jit(solution)/shard_map/ppermute | solution.py:20
  211.1 0.2 rev.26
  211.3 1.4 collective-permute-done.7
  212.7 0.2 rev.27
  213.1 1.4 negate_multiply_fusion
  214.7 1.9 collective-permute-start.8
  216.6 7.9 %collective-permute-start.9 = (f32[1,1,16,128]{3,2,1,0:T(8,128)S(1)}, f32[1,1,16,128]{3,2,1,0:T(8,128)S(1)}, u32[]{:S(2)}, u32[]{:S(2)}) collective-permute-start(f32[1,1,16,128]{3,2,1,0:T(8,128)S(1)} %get-tuple-element.49), channel_id=1, source_target_pairs={{32,0},{64,32},{96,64},{128,96},{160,128},{192,160},{224,192},{256... | collective-permute-start | bytes 24584 | tf_op jit(solution)/shard_map/ppermute | solution.py:21
  224.5 1.3 collective-permute-done.9
  225.9 9.4 %collective-permute-start.10 = (f32[1,34,1,128]{3,2,1,0:T(1,128)S(1)}, f32[1,34,1,128]{3,2,1,0:T(1,128)S(1)}, u32[]{:S(2)}, u32[]{:S(2)}) collective-permute-start(f32[1,34,1,128]{3,2,1,0:T(1,128)S(1)} %get-tuple-element.30), channel_id=1, source_target_pairs={{0,1},{1,2},{2,3},{3,4},{4,5},{5,6},{6,7},{7,8},{8,9},{9,10},{10,1... | collective-permute-start | bytes 52232 | tf_op jit(solution)/shard_map/ppermute | solution.py:20
  235.2 1.9 collective-permute-start.11
  237.3 8.7 %collective-permute-done.11 = f32[1,34,1,128]{3,2,1,0:T(1,128)S(1)} collective-permute-done((f32[1,34,1,128]{3,2,1,0:T(1,128)S(1)}, f32[1,34,1,128]{3,2,1,0:T(1,128)S(1)}, u32[]{:S(2)}, u32[]{:S(2)}) %collective-permute-start.11) | collective-permute-done | bytes 17440 | tf_op jit(solution)/shard_map/ppermute | solution.py:21
  246.2 0.9 bitcast_add_fusion
  247.3 1.9 collective-permute-start.13
  249.3 7.9 %collective-permute-start.12 = (f32[1,1,16,128]{3,2,1,0:T(8,128)S(1)}, f32[1,1,16,128]{3,2,1,0:T(8,128)S(1)}, u32[]{:S(2)}, u32[]{:S(2)}) collective-permute-start(f32[1,1,16,128]{3,2,1,0:T(8,128)S(1)} %get-tuple-element.39), channel_id=1, source_target_pairs={{32,0},{64,32},{96,64},{128,96},{160,128},{192,160},{224,192},{256... | collective-permute-start | bytes 24584 | tf_op jit(solution)/shard_map/ppermute | solution.py:21
  257.3 1.2 collective-permute-done.12
  258.5 1.9 collective-permute-start.15
  260.4 3.9 %collective-permute-start.14 = (f32[1,34,1,128]{3,2,1,0:T(1,128)S(1)}, f32[1,34,1,128]{3,2,1,0:T(1,128)S(1)}, u32[]{:S(2)}, u32[]{:S(2)}) collective-permute-start(f32[1,34,1,128]{3,2,1,0:T(1,128)S(1)} %get-tuple-element.29), channel_id=1, source_target_pairs={{1,0},{2,1},{3,2},{4,3},{5,4},{6,5},{7,6},{8,7},{9,8},{10,9},{11,1... | collective-permute-start | bytes 52232 | tf_op jit(solution)/shard_map/ppermute | solution.py:21
  264.6 6.6 %collective-permute-done.14 = f32[1,34,1,128]{3,2,1,0:T(1,128)S(1)} collective-permute-done((f32[1,34,1,128]{3,2,1,0:T(1,128)S(1)}, f32[1,34,1,128]{3,2,1,0:T(1,128)S(1)}, u32[]{:S(2)}, u32[]{:S(2)}) %collective-permute-start.14) | collective-permute-done | bytes 17440 | tf_op jit(solution)/shard_map/ppermute | solution.py:21
  271.5 1.0 fusion.22
  (89 shorter events, 2.7 us)
Async XLA Ops:
  0.6 1.0 copy-start.11
  2.7 37.3 %all-to-all-start.1 = ((f32[32,1,32]{2,1,0:T(1,128)}), f32[32,1,32]{2,1,0:T(1,128)S(1)}, u32[]{:S(2)}, u32[]{:S(2)}) async-start(f32[32,1,32]{2,1,0:T(1,128)} %bitcast.10), calls=%async_computation.1 | async-start | bytes 32768 | tf_op jit(solution)/shard_map/all_to_all | solution.py:100
  19.6 7.0 %copy-start = (f32[3,32,16,128]{3,2,1,0:T(8,128)S(1)}, f32[3,32,16,128]{3,2,1,0:T(8,128)}, u32[]{:S(2)}) copy-start(f32[3,32,16,128]{3,2,1,0:T(8,128)} %param.17) | copy-start | bytes 2359300
  20.5 6.1 %copy-start.1 = (f32[32,16,128]{2,1,0:T(8,128)S(1)}, f32[32,16,128]{2,1,0:T(8,128)}, u32[]{:S(2)}) copy-start(f32[32,16,128]{2,1,0:T(8,128)} %param.18) | copy-start | bytes 786436
  20.5 129.5 %collective-permute-start = (f32[4,1,16,128]{3,2,1,0:T(8,128)S(1)}, f32[4,1,16,128]{3,2,1,0:T(8,128)S(1)}, u32[]{:S(2)}, u32[]{:S(2)}) collective-permute-start(f32[4,1,16,128]{3,2,1,0:T(8,128)S(1)} %fusion.51), channel_id=1, source_target_pairs={{32,0},{64,32},{96,64},{128,96},{160,128},{192,160},{224,192},{256... | collective-permute-start | bytes 98312 | tf_op jit(solution)/shard_map/ppermute | solution.py:21
  29.0 1.2 copy-start.13
  29.0 1.2 slice-start
  33.3 1.3 copy-start.17
  34.6 1.0 copy-start.9
  34.6 1.0 copy-start.10
  35.6 1.2 copy-start.5
  35.6 1.8 copy-start.3
  40.0 14.7 %copy-start.14 = (s32[1,1,2]{2,1,0:T(1,128)S(1)}, s32[1,1,2]{2,1,0:T(1,128)}, u32[]{:S(2)}) copy-start(s32[1,1,2]{2,1,0:T(1,128)} %param.21) | copy-start | bytes 28
  40.0 24.1 %all-to-all-start = ((f32[32,1,32]{2,1,0:T(1,128)}), f32[32,1,32]{2,1,0:T(1,128)S(1)}, u32[]{:S(2)}, u32[]{:S(2)}) async-start(f32[32,1,32]{2,1,0:T(1,128)} %bitcast.8), calls=%async_computation | async-start | bytes 32768 | tf_op jit(solution)/shard_map/all_to_all | solution.py:99
  66.2 83.8 %copy-start.16 = (f32[4]{0:T(128)S(1)}, f32[4]{0:T(128)}, u32[]{:S(2)}) copy-start(f32[4]{0:T(128)} %constant.71.clone) | copy-start | bytes 52
  150.0 9.4 %collective-permute-start.1 = (f32[4,1,16,128]{3,2,1,0:T(8,128)S(1)}, f32[4,1,16,128]{3,2,1,0:T(8,128)S(1)}, u32[]{:S(2)}, u32[]{:S(2)}) collective-permute-start(f32[4,1,16,128]{3,2,1,0:T(8,128)S(1)} %get-tuple-element.7), channel_id=1, source_target_pairs={{0,32},{32,64},{64,96},{96,128},{128,160},{160,192},{192,224},{224... | collective-permute-start | bytes 98312 | tf_op jit(solution)/shard_map/ppermute | solution.py:20
  152.2 0.7 copy-start.12
  159.6 11.3 %copy-start.15 = (f32[4]{0:T(128)S(1)}, f32[4]{0:T(128)}, u32[]{:S(2)}) copy-start(f32[4]{0:T(128)} %constant.70.clone) | copy-start | bytes 52
  159.6 12.4 %collective-permute-start.2 = (f32[4,34,1,128]{3,2,1,0:T(1,128)S(1)}, f32[4,34,1,128]{3,2,1,0:T(1,128)S(1)}, u32[]{:S(2)}, u32[]{:S(2)}) collective-permute-start(f32[4,34,1,128]{3,2,1,0:T(1,128)S(1)} %get-tuple-element.8), channel_id=1, source_target_pairs={{0,1},{1,2},{2,3},{3,4},{4,5},{5,6},{6,7},{7,8},{8,9},{9,10},{10,1... | collective-permute-start | bytes 208904 | tf_op jit(solution)/shard_map/ppermute | solution.py:20
  168.9 11.4 %collective-permute-start.3 = (f32[4,34,1,128]{3,2,1,0:T(1,128)S(1)}, f32[4,34,1,128]{3,2,1,0:T(1,128)S(1)}, u32[]{:S(2)}, u32[]{:S(2)}) collective-permute-start(f32[4,34,1,128]{3,2,1,0:T(1,128)S(1)} %get-tuple-element.9), channel_id=1, source_target_pairs={{1,0},{2,1},{3,2},{4,3},{5,4},{6,5},{7,6},{8,7},{9,8},{10,9},{11,1... | collective-permute-start | bytes 208904 | tf_op jit(solution)/shard_map/ppermute | solution.py:21
  180.6 1.4 copy-start.8
  180.7 1.3 copy-start.7
  180.7 1.3 copy-start.2
  180.8 1.6 copy-start.4
  180.8 1.7 copy-start.6
  188.6 9.9 %collective-permute-start.5 = (f32[3,1,16,128]{3,2,1,0:T(8,128)S(1)}, f32[3,1,16,128]{3,2,1,0:T(8,128)S(1)}, u32[]{:S(2)}, u32[]{:S(2)}) collective-permute-start(f32[3,1,16,128]{3,2,1,0:T(8,128)S(1)} %get-tuple-element.22), channel_id=1, source_target_pairs={{0,32},{32,64},{64,96},{96,128},{128,160},{160,192},{192,224},{224... | collective-permute-start | bytes 73736 | tf_op jit(solution)/shard_map/ppermute | solution.py:20
  190.5 9.4 %collective-permute-start.4 = (f32[3,1,16,128]{3,2,1,0:T(8,128)S(1)}, f32[3,1,16,128]{3,2,1,0:T(8,128)S(1)}, u32[]{:S(2)}, u32[]{:S(2)}) collective-permute-start(f32[3,1,16,128]{3,2,1,0:T(8,128)S(1)} %get-tuple-element.23), channel_id=1, source_target_pairs={{32,0},{64,32},{96,64},{128,96},{160,128},{192,160},{224,192},{256... | collective-permute-start | bytes 73736 | tf_op jit(solution)/shard_map/ppermute | solution.py:21
  200.0 11.1 %collective-permute-start.6 = (f32[3,34,1,128]{3,2,1,0:T(1,128)S(1)}, f32[3,34,1,128]{3,2,1,0:T(1,128)S(1)}, u32[]{:S(2)}, u32[]{:S(2)}) collective-permute-start(f32[3,34,1,128]{3,2,1,0:T(1,128)S(1)} %get-tuple-element.14), channel_id=1, source_target_pairs={{1,0},{2,1},{3,2},{4,3},{5,4},{6,5},{7,6},{8,7},{9,8},{10,9},{11,1... | collective-permute-start | bytes 156680 | tf_op jit(solution)/shard_map/ppermute | solution.py:21
  201.9 10.8 %collective-permute-start.7 = (f32[3,34,1,128]{3,2,1,0:T(1,128)S(1)}, f32[3,34,1,128]{3,2,1,0:T(1,128)S(1)}, u32[]{:S(2)}, u32[]{:S(2)}) collective-permute-start(f32[3,34,1,128]{3,2,1,0:T(1,128)S(1)} %get-tuple-element.15), channel_id=1, source_target_pairs={{0,1},{1,2},{2,3},{3,4},{4,5},{5,6},{6,7},{7,8},{8,9},{9,10},{10,1... | collective-permute-start | bytes 156680 | tf_op jit(solution)/shard_map/ppermute | solution.py:20
  214.7 9.8 %collective-permute-start.8 = (f32[1,1,16,128]{3,2,1,0:T(8,128)S(1)}, f32[1,1,16,128]{3,2,1,0:T(8,128)S(1)}, u32[]{:S(2)}, u32[]{:S(2)}) collective-permute-start(f32[1,1,16,128]{3,2,1,0:T(8,128)S(1)} %get-tuple-element.48), channel_id=1, source_target_pairs={{0,32},{32,64},{64,96},{96,128},{128,160},{160,192},{192,224},{224... | collective-permute-start | bytes 24584 | tf_op jit(solution)/shard_map/ppermute | solution.py:20
  216.6 9.2 %collective-permute-start.9 = (f32[1,1,16,128]{3,2,1,0:T(8,128)S(1)}, f32[1,1,16,128]{3,2,1,0:T(8,128)S(1)}, u32[]{:S(2)}, u32[]{:S(2)}) collective-permute-start(f32[1,1,16,128]{3,2,1,0:T(8,128)S(1)} %get-tuple-element.49), channel_id=1, source_target_pairs={{32,0},{64,32},{96,64},{128,96},{160,128},{192,160},{224,192},{256... | collective-permute-start | bytes 24584 | tf_op jit(solution)/shard_map/ppermute | solution.py:21
  225.9 11.3 %collective-permute-start.10 = (f32[1,34,1,128]{3,2,1,0:T(1,128)S(1)}, f32[1,34,1,128]{3,2,1,0:T(1,128)S(1)}, u32[]{:S(2)}, u32[]{:S(2)}) collective-permute-start(f32[1,34,1,128]{3,2,1,0:T(1,128)S(1)} %get-tuple-element.30), channel_id=1, source_target_pairs={{0,1},{1,2},{2,3},{3,4},{4,5},{5,6},{6,7},{7,8},{8,9},{9,10},{10,1... | collective-permute-start | bytes 52232 | tf_op jit(solution)/shard_map/ppermute | solution.py:20
  235.2 10.8 %collective-permute-start.11 = (f32[1,34,1,128]{3,2,1,0:T(1,128)S(1)}, f32[1,34,1,128]{3,2,1,0:T(1,128)S(1)}, u32[]{:S(2)}, u32[]{:S(2)}) collective-permute-start(f32[1,34,1,128]{3,2,1,0:T(1,128)S(1)} %get-tuple-element.31), channel_id=1, source_target_pairs={{1,0},{2,1},{3,2},{4,3},{5,4},{6,5},{7,6},{8,7},{9,8},{10,9},{11,1... | collective-permute-start | bytes 52232 | tf_op jit(solution)/shard_map/ppermute | solution.py:21
  247.3 9.9 %collective-permute-start.13 = (f32[1,1,16,128]{3,2,1,0:T(8,128)S(1)}, f32[1,1,16,128]{3,2,1,0:T(8,128)S(1)}, u32[]{:S(2)}, u32[]{:S(2)}) collective-permute-start(f32[1,1,16,128]{3,2,1,0:T(8,128)S(1)} %get-tuple-element.38), channel_id=1, source_target_pairs={{0,32},{32,64},{64,96},{96,128},{128,160},{160,192},{192,224},{224... | collective-permute-start | bytes 24584 | tf_op jit(solution)/shard_map/ppermute | solution.py:20
  249.3 9.2 %collective-permute-start.12 = (f32[1,1,16,128]{3,2,1,0:T(8,128)S(1)}, f32[1,1,16,128]{3,2,1,0:T(8,128)S(1)}, u32[]{:S(2)}, u32[]{:S(2)}) collective-permute-start(f32[1,1,16,128]{3,2,1,0:T(8,128)S(1)} %get-tuple-element.39), channel_id=1, source_target_pairs={{32,0},{64,32},{96,64},{128,96},{160,128},{192,160},{224,192},{256... | collective-permute-start | bytes 24584 | tf_op jit(solution)/shard_map/ppermute | solution.py:21
  258.5 5.9 %collective-permute-start.15 = (f32[1,34,1,128]{3,2,1,0:T(1,128)S(1)}, f32[1,34,1,128]{3,2,1,0:T(1,128)S(1)}, u32[]{:S(2)}, u32[]{:S(2)}) collective-permute-start(f32[1,34,1,128]{3,2,1,0:T(1,128)S(1)} %get-tuple-element.28), channel_id=1, source_target_pairs={{0,1},{1,2},{2,3},{3,4},{4,5},{5,6},{6,7},{7,8},{8,9},{9,10},{10,1... | collective-permute-start | bytes 52232 | tf_op jit(solution)/shard_map/ppermute | solution.py:20
  260.4 10.8 %collective-permute-start.14 = (f32[1,34,1,128]{3,2,1,0:T(1,128)S(1)}, f32[1,34,1,128]{3,2,1,0:T(1,128)S(1)}, u32[]{:S(2)}, u32[]{:S(2)}) collective-permute-start(f32[1,34,1,128]{3,2,1,0:T(1,128)S(1)} %get-tuple-element.29), channel_id=1, source_target_pairs={{1,0},{2,1},{3,2},{4,3},{5,4},{6,5},{7,6},{8,7},{9,8},{10,9},{11,1... | collective-permute-start | bytes 52232 | tf_op jit(solution)/shard_map/ppermute | solution.py:21
where the time goes:
time: 273 us; the launch traced here: 272 us
  starting transfers between devices  108 us (40%)
  blocking collectives  83.8 us (31%)
  waiting for transfers between devices  36.2 us (13%)
  other arithmetic  23.4 us (9%)
  local copies, waits for them, and re-layouts  14.4 us (5%)
  between operations  3.77 us (1%)
    unnamed x1, blocking collectives  83.8 us
    ppermute x8, starting transfers between devices, extended(): after = lax.ppermute(initial, axis, down)  39.4 us
    ppermute x8, starting transfers between devices, extended(): before = lax.ppermute(last, axis, up)  37.3 us
    ppermute x8, waiting for transfers between devices, extended(): after = lax.ppermute(initial, axis, down)  27.3 us
    all_to_all x1, starting transfers between devices, body(): lax.all_to_all(send_marks, 'girth', split_axis=0, concat_axis=0, tiled=True)  17 us
    all_to_all x1, starting transfers between devices, body(): lax.all_to_all(send_values, 'girth', split_axis=0, concat_axis=0, tiled=T...  14.7 us
    concatenate x5, other arithmetic, body(): moving = jnp.concatenate([velocity, pressure[None]], axis=0)  5.82 us
  transfers between devices with their start and end apart: 18, of which 10 were waited for; matrix products, arithmetic and copies ran while one was open for 8% of the time, Pallas kernels for 0%

commit v1 on v0

v1 whole, which is shorter than its diff:
```python
import jax
import jax.numpy as jnp
from jax import lax
from jax.experimental import pallas as pl
from jax.experimental.pallas import tpu as pltpu
from jax.sharding import PartitionSpec as P

viscosity = 0.02
thrust = 8.0
target_speed = 0.5

BI, BJ, BK, DMAX = 32, 16, 128, 512
CELLS = BI * BJ
COLS = (3, 4, 3, 4, 3)
COL_AT = (0, 3, 7, 10, 14)
LAYERS = (4, 3, 3, 4, 3)
LAYER_AT = (0, 4, 7, 10, 14)
LIST_ROWS = 12
G_LIST = 17 * BI
G_ROWS = G_LIST + 16
WIDE = BJ + 8
S_LIST = 17 * WIDE
S_LOAD = S_LIST + 3 * LIST_ROWS
S_FACE = S_LOAD + 1
S_ROWS = S_LIST + 40
EL, EC = BI + 8, 48
LO, LO_OUT, LO_IN, OWN, HI_IN, HI_OUT, HI = 10, 14, 15, 16, 32, 33, 34
F32, BF16, I32 = jnp.float32, jnp.bfloat16, jnp.int32


def iota(shape, dim):
    return lax.broadcasted_iota(I32, shape, dim)


def three(x):
    a = x.astype(BF16)
    rest = x - a.astype(F32)
    b = rest.astype(BF16)
    c = (rest - b.astype(F32)).astype(BF16)
    return a, b, c


def wide_row(ref, at):
    return jnp.concatenate([ref[at + q : at + q + 1, :] for q in range(4)], axis=1)


def put_row(ref, at, row):
    for q in range(4):
        ref[at + q : at + q + 1, :] = row[:, q * BK : (q + 1) * BK]


def head_kernel(vel, prs, tk, tw, cells, sector, weight, sums, to_high, to_low):
    def column(f, j):
        rows = pl.ds(j, BI, stride=BJ)
        if f < 3:
            return vel[f, rows, :]
        if f == 3:
            return prs[rows, :]
        return viscosity + tk[rows, :] / tw[rows, :]

    for f in range(5):
        n = COLS[f]
        for c in range(n):
            at = (COL_AT[f] + c) * BI
            to_high[at : at + BI, :] = column(f, BJ - n + c)
            to_low[at : at + BI, :] = column(f, c)
    cell = cells[...]
    owner = sector[...]
    for ref in (to_high, to_low):
        put_row(ref, G_LIST, cell.astype(F32))
        put_row(ref, G_LIST + 4, owner.astype(F32))
        put_row(ref, G_LIST + 8, weight[...])
        ref[G_LIST + LIST_ROWS : G_ROWS, :] = jnp.zeros((4, BK), F32)
    pick = jnp.where(iota((CELLS, DMAX), 0) == cell // BK, 1.0, 0.0).astype(BF16)
    parts = jnp.concatenate(three(vel[0]), axis=1)
    found = lax.dot_general(parts, pick, (((0,), (0,)), ((), ())), preferred_element_type=F32)
    found = found[:BK] + found[BK : 2 * BK] + found[2 * BK :]
    inflow = jnp.sum(jnp.where(iota((BK, DMAX), 0) == cell % BK, found, 0.0), axis=0, keepdims=True)
    mine = iota((64, DMAX), 0)
    both = jnp.where(mine == owner, inflow, 0.0) + jnp.where(mine == owner + 32, 1.0, 0.0)
    both = jnp.concatenate([both, jnp.zeros((64, DMAX), F32)], axis=0)
    total = lax.dot_general(
        jnp.ones((8, DMAX), F32),
        both,
        (((1,), (1,)), ((), ())),
        precision=lax.Precision.HIGHEST,
        preferred_element_type=F32,
    )
    for t in range(sums.shape[0] // 8):
        sums[t * 8 : t * 8 + 8, :] = total


def middle_kernel(vel, prs, tk, tw, cells, sector, weight, face, from_low, from_high, sums, up, down, load):
    for f in range(5):
        n, m = LAYERS[f], COLS[f]
        for q in range(n):
            for ref, i in ((up, BI - n + q), (down, q)):
                at = (LAYER_AT[f] + q) * WIDE
                rows = pl.ds(i * BJ, BJ)
                if f < 3:
                    own = vel[f, rows, :]
                elif f == 3:
                    own = prs[rows, :]
                else:
                    own = viscosity + tk[rows, :] / tw[rows, :]
                ref[at : at + BJ, :] = own
                for c in range(m):
                    row = (COL_AT[f] + c) * BI + i
                    low_at, high_at = at + BJ + 4 - m + c, at + BJ + 4 + c
                    ref[low_at : low_at + 1, :] = from_low[row : row + 1, :]
                    ref[high_at : high_at + 1, :] = from_high[row : row + 1, :]
    total = jnp.sum(sums[...], axis=0, keepdims=True)
    filled = pltpu.roll(jnp.broadcast_to(total, (8, BK)), BK - 32, 1)[:1]
    value = thrust * (target_speed - total / jnp.maximum(filled, 1.0))
    value = jnp.where(iota((1, BK), 1) < 32, value, 0.0)
    load[...] = jnp.broadcast_to(value, (8, BK))
    lane = iota((1, BK), 1)
    sides = jnp.where(lane == 0, face[0], jnp.where(lane == 1, face[1], 0)).astype(F32)
    for ref in (up, down):
        put_row(ref, S_LIST, cells[...].astype(F32))
        put_row(ref, S_LIST + 4, sector[...].astype(F32))
        put_row(ref, S_LIST + 8, weight[...])
        ref[S_LIST + 12 : S_LIST + 24, :] = from_low[G_LIST : G_LIST + 12, :]
        ref[S_LIST + 24 : S_LIST + 36, :] = from_high[G_LIST : G_LIST + 12, :]
        ref[S_LOAD : S_LOAD + 1, :] = value
        ref[S_FACE : S_FACE + 1, :] = sides
        ref[S_FACE + 1 : S_ROWS, :] = jnp.zeros((S_ROWS - S_FACE - 1, BK), F32)


def spread_list(cell, owner, weight, load, row, count):
    mine = jnp.where(iota((BK, DMAX), 0) == owner, 1.0, 0.0)
    given = jnp.dot(load, mine, precision=lax.Precision.HIGHEST, preferred_element_type=F32)[:1] * weight
    value = jnp.where(iota((BK, DMAX), 0) == cell % BK, given, 0.0)
    parts = jnp.concatenate(three(value), axis=0)
    pick = jnp.where(iota((count, DMAX), 0) == row, 1.0, 0.0).astype(BF16)
    out = lax.dot_general(pick, parts, (((1,), (1,)), ((), ())), preferred_element_type=F32)
    return out[:, :BK] + out[:, BK : 2 * BK] + out[:, 2 * BK :]


def tail_kernel(vel, prs, tk, tw, cells, sector, weight, face, place, from_low, from_high, from_up, from_down, load, vel_out, prs_out, *scratch):
    block = scratch[:5]
    star = scratch[5:8]
    force, sweep, second = scratch[8:11]
    first_row = place[0] == 0
    last_row = place[0] == place[1] - 1

    def flat(ref):
        return ref.reshape(EL * EC, BK)

    for f in range(5):
        to = block[f]
        if f < 3:
            own = vel[f]
        elif f == 3:
            own = prs[...]
        else:
            own = viscosity + tk[...] / tw[...]
        to[4 : 4 + BI, OWN : OWN + BJ, :] = own.reshape(BI, BJ, BK)
        m, n = COLS[f], LAYERS[f]
        lines = flat(to)
        for c in range(m):
            at = (COL_AT[f] + c) * BI
            lines[pl.ds(4 * EC + LO + 4 - m + c, BI, stride=EC), :] = from_low[at : at + BI, :]
            lines[pl.ds(4 * EC + HI + c, BI, stride=EC), :] = from_high[at : at + BI, :]
        for q in range(n):
            at = (LAYER_AT[f] + q) * WIDE
            for ref, layer in ((from_up, 4 - n + q), (from_down, 4 + BI + q)):
                to[layer, OWN : OWN + BJ, :] = ref[at : at + BJ, :]
                to[layer, LO : LO + 4, :] = ref[at + BJ : at + BJ + 4, :]
                to[layer, HI : HI + 4, :] = ref[at + BJ + 4 : at + BJ + 8, :]

    layer = iota((EL, BK), 0)
    up_face = from_up[S_FACE : S_FACE + 1, :]
    down_face = from_down[S_FACE : S_FACE + 1, :]

    def turned(side):
        own = face[side].astype(F32)
        above = jnp.broadcast_to(up_face[:, side : side + 1], (EL, BK))
        below = jnp.broadcast_to(down_face[:, side : side + 1], (EL, BK))
        return jnp.where(layer < 4, above, jnp.where(layer < 4 + BI, own, below)) > 0.5

    low_turned, high_turned = turned(0), turned(1)
    backward = BK - 1 - iota((EL, BK), 1)

    def images(ref, outer=True):
        lines = flat(ref)
        for source, target, mask in (
            (LO + 3, LO_IN, low_turned),
            (HI, HI_IN, high_turned),
            (OWN, LO_OUT, low_turned),
            (OWN + BJ - 1, HI_OUT, high_turned),
        )[: 4 if outer else 2]:
            value = lines[pl.ds(source, EL, stride=EC), :]
            mirror = jnp.take_along_axis(value, backward, axis=1, mode="promise_in_bounds")
            lines[pl.ds(target, EL, stride=EC), :] = jnp.where(mask, mirror, value)

    @pl.when(first_row)
    def _():
        for f in range(3):
            block[f][3] = jnp.zeros((EC, BK), F32)
        block[3][3] = block[3][4]

    @pl.when(last_row)
    def _():
        for f in range(3):
            block[f][4 + BI] = block[f][3 + BI]
        block[3][4 + BI] = jnp.zeros((EC, BK), F32)

    for f in range(4):
        images(block[f])

    own_load = load[...]
    lists = {}
    lists[0, 0] = (cells[...], sector[...], weight[...], own_load)
    for d, ref in ((-1, from_low), (1, from_high)):
        lists[0, d] = tuple(wide_row(ref, G_LIST + 4 * q) for q in range(3)) + (own_load,)
    for s, ref in ((-1, from_up), (1, from_down)):
        there = jnp.broadcast_to(ref[S_LOAD : S_LOAD + 1, :], (8, BK))
        for n, d in enumerate((0, -1, 1)):
            at = S_LIST + LIST_ROWS * n
            lists[s, d] = tuple(wide_row(ref, at + 4 * q) for q in range(3)) + (there,)
    lines = flat(force)
    for (s, d), (cell, owner, share, there) in lists.items():
        cell, owner = cell.astype(I32), owner.astype(I32)
        i, j = cell // (BJ * BK), (cell // BK) % BJ
        depth = {-1: BI - 3, 0: 0, 1: 0}[s]
        if s == 0 and d == 0:
            out = spread_list(cell, owner, share, there, cell // BK, CELLS)
            force[4 : 4 + BI, OWN : OWN + BJ, :] = out.reshape(BI, BJ, BK)
        elif s == 0:
            j0 = BJ - 2 if d < 0 else 0
            row = jnp.where((j >= j0) & (j < j0 + 2), (j - j0) * BI + i, -1)
            out = spread_list(cell, owner, share, there, row, 2 * BI)
            for c in range(2):
                at = 4 * EC + (LO + 2 if d < 0 else HI) + c
                lines[pl.ds(at, BI, stride=EC), :] = out[c * BI : (c + 1) * BI]
        elif d == 0:
            row = jnp.where((i >= depth) & (i < depth + 3), (i - depth) * BJ + j, -1)
            out = spread_list(cell, owner, share, there, row, 3 * BJ)
            at = 1 if s < 0 else 4 + BI
            force[at : at + 3, OWN : OWN + BJ, :] = out.reshape(3, BJ, BK)
        else:
            i0 = BI - 2 if s < 0 else 0
            j0 = BJ - 2 if d < 0 else 0
            row = jnp.where((i >= i0) & (i < i0 + 2) & (j >= j0) & (j < j0 + 2), (i - i0) * 2 + (j - j0), -1)
            out = spread_list(cell, owner, share, there, row, 8)
            at = 2 if s < 0 else 4 + BI
            to = LO + 2 if d < 0 else HI
            for q in range(2):
                force[at + q, to : to + 2, :] = out[2 * q : 2 * q + 2]

    lane = iota((32, BK), 1)

    def below(x, sign):
        return jnp.where(lane[: x.shape[0]] == 0, sign * x, pltpu.roll(x, 1, 1))

    def above(x):
        return jnp.where(lane[: x.shape[0]] == BK - 1, 0.0, pltpu.roll(x, BK - 1, 1))

    mid, left, right = slice(8, 40), slice(7, 39), slice(9, 41)

    def star_step(l, carry):
        e = block[4][l, mid, :]
        share = 1.0 / (1.0 + 3.0 * e)
        half = 0.5 * e
        p = block[3]
        q = p[l, mid, :]
        slope = (
            p[l + 1, mid, :] - p[l - 1, mid, :],
            p[l, right, :] - p[l, left, :],
            above(q) - below(q, 1.0),
        )
        for c in range(3):
            u = block[c]
            x, a, b = u[l, mid, :], u[l - 1, mid, :], u[l + 1, mid, :]
            around = a + b + u[l, left, :] + u[l, right, :] + below(x, -1.0) + above(x)
            value = x - 0.125 * (b - a) + half * around - 0.25 * slope[c]
            if c == 0:
                value = value + 0.5 * force[l, mid, :]
            star[c][l, mid, :] = value * share
        return carry

    lax.fori_loop(1, EL - 1, star_step, 0)

    @pl.when(first_row)
    def _():
        star[0][3] = jnp.zeros((EC, BK), F32)

    @pl.when(last_row)
    def _():
        star[0][4 + BI] = star[0][3 + BI]

    images(star[1])

    def sweep_step(l, carry):
        x = star[2][l, mid, :]
        total = (star[0][l + 1, mid, :] - star[0][l - 1, mid, :]) + (star[1][l, right, :] - star[1][l, left, :])
        sweep[l, mid, :] = (total + (above(x) - below(x, -1.0))) * (-1.0 / 6.0)
        return carry

    lax.fori_loop(2, EL - 2, sweep_step, 0)

    @pl.when(first_row)
    def _():
        sweep[3] = sweep[4]

    @pl.when(last_row)
    def _():
        sweep[4 + BI] = jnp.zeros((EC, BK), F32)

    images(sweep)

    def second_step(l, carry):
        x = sweep[l, mid, :]
        around = sweep[l - 1, mid, :] + sweep[l + 1, mid, :] + sweep[l, left, :] + sweep[l, right, :]
        second[l, mid, :] = (around + below(x, 1.0) + above(x)) * (1.0 / 6.0) + x
        return carry

    lax.fori_loop(3, EL - 3, second_step, 0)

    @pl.when(first_row)
    def _():
        second[3] = second[4]

    @pl.when(last_row)
    def _():
        second[4 + BI] = jnp.zeros((EC, BK), F32)

    images(second, outer=False)
    own, own_left, own_right = slice(OWN, OWN + BJ), slice(OWN - 1, OWN + BJ - 1), slice(OWN + 1, OWN + BJ + 1)

    def out_step(i, carry):
        l = i + 4
        x = second[l, own, :]
        slope = (
            second[l + 1, own, :] - second[l - 1, own, :],
            second[l, own_right, :] - second[l, own_left, :],
            above(x) - below(x, 1.0),
        )
        for c in range(3):
            vel_out[c, i] = star[c][l, own, :] - 0.25 * slope[c]
        prs_out[i] = block[3][l, own, :] + x
        return carry

    lax.fori_loop(0, BI, out_step, 0)


def body(velocity, pressure, turb_k, turb_omega, face_code, disc_cells, disc_sector, disc_weight):
    streams, girths = lax.axis_size("stream"), lax.axis_size("girth")
    vmem = pl.BlockSpec(memory_space=pltpu.VMEM)
    smem = pl.BlockSpec(memory_space=pltpu.SMEM)
    params = pltpu.CompilerParams(vmem_limit_bytes=48 * 2**20)
    vel = velocity.reshape(3, CELLS, BK)
    prs, tk, tw = (x.reshape(CELLS, BK) for x in (pressure, turb_k, turb_omega))
    cells, sector, weight = disc_cells, disc_sector.reshape(1, DMAX), disc_weight
    face = face_code.reshape(2)
    place = jnp.stack([lax.axis_index("stream").astype(I32), jnp.int32(streams)])
    fields = (vel, prs, tk, tw, cells, sector, weight)

    g_pack = jax.ShapeDtypeStruct((G_ROWS, BK), F32)
    sums, to_high, to_low = pl.pallas_call(
        head_kernel,
        out_shape=(jax.ShapeDtypeStruct((girths, BK), F32), g_pack, g_pack),
        in_specs=[vmem] * 7,
        out_specs=(vmem,) * 3,
        compiler_params=params,
        name="head",
    )(*fields)
    ring = [(g, (g + 1) % girths) for g in range(girths)]
    from_low = lax.ppermute(to_high, "girth", ring)
    from_high = lax.ppermute(to_low, "girth", [(b, a) for a, b in ring])
    sums = lax.all_to_all(sums, "girth", split_axis=0, concat_axis=0, tiled=True)

    s_pack = jax.ShapeDtypeStruct((S_ROWS, BK), F32)
    up, down, load = pl.pallas_call(
        middle_kernel,
        out_shape=(s_pack, s_pack, jax.ShapeDtypeStruct((8, BK), F32)),
        in_specs=[vmem] * 7 + [smem] + [vmem] * 3,
        out_specs=(vmem,) * 3,
        compiler_params=params,
        name="middle",
    )(*fields, face, from_low, from_high, sums)
    chain = [(s, s + 1) for s in range(streams - 1)]
    from_up = lax.ppermute(up, "stream", chain)
    from_down = lax.ppermute(down, "stream", [(b, a) for a, b in chain])

    return pl.pallas_call(
        tail_kernel,
        out_shape=(
            jax.ShapeDtypeStruct((3, BI, BJ, BK), F32),
            jax.ShapeDtypeStruct((BI, BJ, BK), F32),
        ),
        in_specs=[vmem] * 7 + [smem] * 2 + [vmem] * 5,
        out_specs=(vmem,) * 2,
        scratch_shapes=[pltpu.VMEM((EL, EC, BK), F32)] * 11,
        compiler_params=params,
        name="tail",
    )(*fields, face, place, from_low, from_high, from_up, from_down, load)


def solution(mesh):
    block = P("stream", "girth", None)
    placed = (P(None, "stream", "girth", None), block, block, block, block, P("stream", "girth"), block, P("stream", "girth"))
    return jax.shard_map(
        body,
        mesh=mesh,
        in_specs=placed,
        out_specs=(P(None, "stream", "girth", None), block),
        check_vma=False,
    )
```

time: 273 us -> 80 us (0.29)
  the two profiles are of different devices: /device:TPU:248 before, /device:TPU:1 now
where the time goes in v1:
time: 80 us; the launch traced here: 79.6 us
  starting transfers between devices  27.2 us (34%)
  blocking collectives  20.8 us (26%)
  Pallas kernels  19.5 us (24%)
  waiting for transfers between devices  5.94 us (7%)
  local copies, waits for them, and re-layouts  5.34 us (7%)
    all_to_all x1, blocking collectives, body(): lax.all_to_all(sums, 'girth', split_axis=0, concat_axis=0, tiled=True)  20.8 us
    pallas_call x1, Pallas kernels, body(): pl.pallas_call(tail_kernel, out_shape=(jax.ShapeDtypeStruct((3, BI, BJ, B...  18 us
    ppermute x1, starting transfers between devices, body(): from_high = lax.ppermute(to_low, 'girth', [(b, a) for a, b in ring])  15.9 us
    ppermute x1, starting transfers between devices, body(): from_up = lax.ppermute(up, 'stream', chain)  5.37 us
    unnamed x24, local copies, waits for them, and re-layouts  5.34 us
    ppermute x1, waiting for transfers between devices, body(): from_down = lax.ppermute(down, 'stream', [(b, a) for a, b in chain])  5.01 us
    ppermute x1, starting transfers between devices, body(): from_low = lax.ppermute(to_high, 'girth', ring)  4.05 us
    ppermute x1, starting transfers between devices, body(): from_down = lax.ppermute(down, 'stream', [(b, a) for a, b in chain])  1.92 us
  transfers between devices with their start and end apart: 4, of which 2 were waited for; matrix products, arithmetic and copies ran while one was open for 0% of the time, Pallas kernels for 0%

profile of v1, /device:TPU:1, one launch (start us, length us, event | category | flops | bytes accessed | tf_op | source)
XLA Modules:
  0.0 79.6 jit_solution(2204773034021092719)
XLA Ops:
  0.6 0.0 copy-start.10
  0.6 0.0 copy-start.9
  0.7 0.0 copy-start.8
  0.7 0.7 copy-done.10
  1.3 0.0 copy-done.9
  1.3 0.0 copy-done.8
  1.3 0.0 copy-start
  1.3 1.1 %copy-done = f32[3,32,16,128]{3,2,1,0:T(8,128)S(1)} copy-done((f32[3,32,16,128]{3,2,1,0:T(8,128)S(1)}, f32[3,32,16,128]{3,2,1,0:T(8,128)}, u32[]{:S(2)}) %copy-start) | copy-done | bytes 786456
  2.5 0.0 copy-start.2
  2.5 0.9 %copy-done.2 = f32[32,16,128]{2,1,0:T(8,128)S(1)} copy-done((f32[32,16,128]{2,1,0:T(8,128)S(1)}, f32[32,16,128]{2,1,0:T(8,128)}, u32[]{:S(2)}) %copy-start.2) | copy-done | bytes 262168
  3.4 0.0 copy-start.4
  3.4 0.9 %copy-done.4 = f32[32,16,128]{2,1,0:T(8,128)S(1)} copy-done((f32[32,16,128]{2,1,0:T(8,128)S(1)}, f32[32,16,128]{2,1,0:T(8,128)}, u32[]{:S(2)}) %copy-start.4) | copy-done | bytes 262168
  4.4 0.0 copy-start.6
  4.4 0.9 %copy-done.6 = f32[32,16,128]{2,1,0:T(8,128)S(1)} copy-done((f32[32,16,128]{2,1,0:T(8,128)S(1)}, f32[32,16,128]{2,1,0:T(8,128)}, u32[]{:S(2)}) %copy-start.6) | copy-done | bytes 262168
  5.3 0.8 head.1
  6.1 4.1 %collective-permute-start = (f32[560,128]{1,0:T(8,128)S(1)}, f32[560,128]{1,0:T(8,128)S(1)}, u32[]{:S(2)}, u32[]{:S(2)}) collective-permute-start(f32[560,128]{1,0:T(8,128)S(1)} %get-tuple-element.8), channel_id=1, source_target_pairs={{0,1},{1,2},{2,3},{3,4},{4,5},{5,6},{6,7},{7,8},{8,9},{9,10},{10,1... | collective-permute-start | bytes 860168 | tf_op jit(solution)/shard_map/ppermute | solution.py:370
  10.2 15.9 %collective-permute-start.1 = (f32[560,128]{1,0:T(8,128)S(1)}, f32[560,128]{1,0:T(8,128)S(1)}, u32[]{:S(2)}, u32[]{:S(2)}) collective-permute-start(f32[560,128]{1,0:T(8,128)S(1)} %get-tuple-element.9), channel_id=1, source_target_pairs={{1,0},{2,1},{3,2},{4,3},{5,4},{6,5},{7,6},{8,7},{9,8},{10,9},{11,1... | collective-permute-start | bytes 860168 | tf_op jit(solution)/shard_map/ppermute | solution.py:371
  26.1 20.8 %all_to_all.11 = f32[32,1,128]{2,1,0:T(1,128)S(1)} all-to-all(f32[32,1,128]{2,1,0:T(1,128)S(1)} %bitcast.27), channel_id=1, replica_groups=mesh['stream'=24,'girth'=32] {'girth'}, dimensions={0} | all-to-all | bytes 32768 | tf_op jit(solution)/shard_map/all_to_all | solution.py:372
  46.8 0.0 collective-permute-done.from_low
  46.8 0.0 collective-permute-done.1.from_high
  46.8 0.0 copy-start.11
  46.8 0.7 copy-done.11
  47.5 0.0 copy-start.1
  47.5 0.0 copy-start.3
  47.5 0.0 copy-start.5
  47.5 0.0 copy-start.7
  47.5 0.7 middle.1
  48.2 5.4 %collective-permute-start.2 = (f32[448,128]{1,0:T(8,128)S(1)}, f32[448,128]{1,0:T(8,128)S(1)}, u32[]{:S(2)}, u32[]{:S(2)}) collective-permute-start(f32[448,128]{1,0:T(8,128)S(1)} %get-tuple-element.11), channel_id=1, source_target_pairs={{0,32},{32,64},{64,96},{96,128},{128,160},{160,192},{192,224},{224... | collective-permute-start | bytes 688136 | tf_op jit(solution)/shard_map/ppermute | solution.py:384
  53.6 1.9 %collective-permute-start.3 = (f32[448,128]{1,0:T(8,128)S(1)}, f32[448,128]{1,0:T(8,128)S(1)}, u32[]{:S(2)}, u32[]{:S(2)}) collective-permute-start(f32[448,128]{1,0:T(8,128)S(1)} %get-tuple-element.12), channel_id=1, source_target_pairs={{32,0},{64,32},{96,64},{128,96},{160,128},{192,160},{224,192},{256... | collective-permute-start | bytes 688136 | tf_op jit(solution)/shard_map/ppermute | solution.py:385
  55.6 0.1 pad_add_fusion.place
  55.6 0.9 %collective-permute-done.2.from_up = f32[448,128]{1,0:T(8,128)S(1)} collective-permute-done((f32[448,128]{1,0:T(8,128)S(1)}, f32[448,128]{1,0:T(8,128)S(1)}, u32[]{:S(2)}, u32[]{:S(2)}) %collective-permute-start.2) | collective-permute-done | bytes 229408 | tf_op jit(solution)/shard_map/ppermute | solution.py:384
  56.6 5.0 %collective-permute-done.3.from_down = f32[448,128]{1,0:T(8,128)S(1)} collective-permute-done((f32[448,128]{1,0:T(8,128)S(1)}, f32[448,128]{1,0:T(8,128)S(1)}, u32[]{:S(2)}, u32[]{:S(2)}) %collective-permute-start.3) | collective-permute-done | bytes 229408 | tf_op jit(solution)/shard_map/ppermute | solution.py:385
  61.6 0.0 copy-done.1
  61.6 0.0 copy-done.3
  61.6 0.0 copy-done.5
  61.6 0.0 copy-done.7
  61.6 18.0 %tail.1 = (f32[3,32,16,128]{3,2,1,0:T(8,128)}, f32[32,16,128]{2,1,0:T(8,128)}) custom-call(f32[3,512,128]{2,1,0:T(8,128)S(1)} %bitcast.13, f32[512,128]{1,0:T(8,128)S(1)} %bitcast.16, f32[512,128]{1,0:T(8,128)S(1)} %bitcast.19, f32[512,128]{1,0:T(8,128)S(1)} %bitcast.22, s32[1,512]{1,0:T(1,128)S(1)} %copy-done.8, s32[1,512]{1,0:T(1,128)S(1)} %bitcast.26, ...), custom_call_target="tpu_custom_call" | custom-call | tf_op jit(solution)/shard_map/tail/pallas_call | solution.py:387
Async XLA Ops:
  0.6 0.7 copy-start.10
  0.6 0.7 copy-start.9
  0.7 0.7 copy-start.8
  1.3 1.1 %copy-start = (f32[3,32,16,128]{3,2,1,0:T(8,128)S(1)}, f32[3,32,16,128]{3,2,1,0:T(8,128)}, u32[]{:S(2)}) copy-start(f32[3,32,16,128]{3,2,1,0:T(8,128)} %param.8) | copy-start | bytes 2359300
  2.5 0.9 %copy-start.2 = (f32[32,16,128]{2,1,0:T(8,128)S(1)}, f32[32,16,128]{2,1,0:T(8,128)}, u32[]{:S(2)}) copy-start(f32[32,16,128]{2,1,0:T(8,128)} %param.9) | copy-start | bytes 786436
  3.4 0.9 %copy-start.4 = (f32[32,16,128]{2,1,0:T(8,128)S(1)}, f32[32,16,128]{2,1,0:T(8,128)}, u32[]{:S(2)}) copy-start(f32[32,16,128]{2,1,0:T(8,128)} %param.10) | copy-start | bytes 786436
  4.4 0.9 %copy-start.6 = (f32[32,16,128]{2,1,0:T(8,128)S(1)}, f32[32,16,128]{2,1,0:T(8,128)}, u32[]{:S(2)}) copy-start(f32[32,16,128]{2,1,0:T(8,128)} %param.11) | copy-start | bytes 786436
  6.1 40.7 %collective-permute-start = (f32[560,128]{1,0:T(8,128)S(1)}, f32[560,128]{1,0:T(8,128)S(1)}, u32[]{:S(2)}, u32[]{:S(2)}) collective-permute-start(f32[560,128]{1,0:T(8,128)S(1)} %get-tuple-element.8), channel_id=1, source_target_pairs={{0,1},{1,2},{2,3},{3,4},{4,5},{5,6},{6,7},{7,8},{8,9},{9,10},{10,1... | collective-permute-start | bytes 860168 | tf_op jit(solution)/shard_map/ppermute | solution.py:370
  10.2 36.7 %collective-permute-start.1 = (f32[560,128]{1,0:T(8,128)S(1)}, f32[560,128]{1,0:T(8,128)S(1)}, u32[]{:S(2)}, u32[]{:S(2)}) collective-permute-start(f32[560,128]{1,0:T(8,128)S(1)} %get-tuple-element.9), channel_id=1, source_target_pairs={{1,0},{2,1},{3,2},{4,3},{5,4},{6,5},{7,6},{8,7},{9,8},{10,9},{11,1... | collective-permute-start | bytes 860168 | tf_op jit(solution)/shard_map/ppermute | solution.py:371
  46.8 0.7 copy-start.11
  47.5 14.1 %copy-start.1 = (f32[3,32,16,128]{3,2,1,0:T(8,128)S(1)}, f32[3,32,16,128]{3,2,1,0:T(8,128)}, u32[]{:S(2)}) copy-start(f32[3,32,16,128]{3,2,1,0:T(8,128)} %param.8) | copy-start | bytes 2359300
  47.5 14.1 %copy-start.3 = (f32[32,16,128]{2,1,0:T(8,128)S(1)}, f32[32,16,128]{2,1,0:T(8,128)}, u32[]{:S(2)}) copy-start(f32[32,16,128]{2,1,0:T(8,128)} %param.9) | copy-start | bytes 786436
  47.5 14.1 %copy-start.5 = (f32[32,16,128]{2,1,0:T(8,128)S(1)}, f32[32,16,128]{2,1,0:T(8,128)}, u32[]{:S(2)}) copy-start(f32[32,16,128]{2,1,0:T(8,128)} %param.10) | copy-start | bytes 786436
  47.5 14.1 %copy-start.7 = (f32[32,16,128]{2,1,0:T(8,128)S(1)}, f32[32,16,128]{2,1,0:T(8,128)}, u32[]{:S(2)}) copy-start(f32[32,16,128]{2,1,0:T(8,128)} %param.11) | copy-start | bytes 786436
  48.2 8.3 %collective-permute-start.2 = (f32[448,128]{1,0:T(8,128)S(1)}, f32[448,128]{1,0:T(8,128)S(1)}, u32[]{:S(2)}, u32[]{:S(2)}) collective-permute-start(f32[448,128]{1,0:T(8,128)S(1)} %get-tuple-element.11), channel_id=1, source_target_pairs={{0,32},{32,64},{64,96},{96,128},{128,160},{160,192},{192,224},{224... | collective-permute-start | bytes 688136 | tf_op jit(solution)/shard_map/ppermute | solution.py:384
  53.6 8.0 %collective-permute-start.3 = (f32[448,128]{1,0:T(8,128)S(1)}, f32[448,128]{1,0:T(8,128)S(1)}, u32[]{:S(2)}, u32[]{:S(2)}) collective-permute-start(f32[448,128]{1,0:T(8,128)S(1)} %get-tuple-element.12), channel_id=1, source_target_pairs={{32,0},{64,32},{96,64},{128,96},{160,128},{192,160},{224,192},{256... | collective-permute-start | bytes 688136 | tf_op jit(solution)/shard_map/ppermute | solution.py:385

commit v2 on v1

v2 whole, which is shorter than its diff:
```python
import jax
import jax.numpy as jnp
from jax import lax
from jax.experimental import pallas as pl
from jax.experimental.pallas import tpu as pltpu
from jax.sharding import PartitionSpec as P

viscosity = 0.02
thrust = 8.0
target_speed = 0.5

BI, BJ, BK, DMAX = 32, 16, 128, 512
CELLS = BI * BJ
COLS = (3, 4, 3, 4, 3)
COL_AT = (0, 3, 7, 10, 14)
LAYERS = (4, 3, 3, 4, 3)
LAYER_AT = (0, 4, 7, 10, 14)
LIST_ROWS = 12
G_LIST = 17 * BI
G_ROWS = G_LIST + 16
WIDE = BJ + 8
FORCE_AT = 17
S_FACE = 20 * WIDE
S_ROWS = S_FACE + 8
INNER = (8, 32)
EL, EC = BI + 8, 48
LO, LO_OUT, LO_IN, OWN, HI_IN, HI_OUT, HI = 10, 14, 15, 16, 32, 33, 34
F32, BF16, I32 = jnp.float32, jnp.bfloat16, jnp.int32


def iota(shape, dim):
    return lax.broadcasted_iota(I32, shape, dim)


def three(x):
    a = x.astype(BF16)
    rest = x - a.astype(F32)
    b = rest.astype(BF16)
    c = (rest - b.astype(F32)).astype(BF16)
    return a, b, c


def wide_row(ref, at):
    return jnp.concatenate([ref[at + q : at + q + 1, :] for q in range(4)], axis=1)


def lines(ref):
    return ref.reshape(EL * EC, BK)


def put_row(ref, at, row):
    for q in range(4):
        ref[at + q : at + q + 1, :] = row[:, q * BK : (q + 1) * BK]


def head_kernel(vel, prs, tk, tw, cells, sector, weight, face, *refs):
    block, (sums, to_high, to_low, info) = refs[:5], refs[5:9]
    k_buf, w_buf, cell_buf, owner_buf, share_buf, face_buf, sem = refs[9:]
    inside = (slice(4, 4 + BI), slice(OWN, OWN + BJ))
    pairs = (
        (cells, cell_buf),
        (sector, owner_buf),
        (weight, share_buf),
        (face, face_buf),
        (vel.at[0], block[0].at[inside]),
        (vel.at[1], block[1].at[inside]),
        (vel.at[2], block[2].at[inside]),
        (prs, block[3].at[inside]),
        (tk, k_buf),
        (tw, w_buf),
    )
    copies = [pltpu.make_async_copy(a, b, sem.at[n]) for n, (a, b) in enumerate(pairs)]
    for copy in copies:
        copy.start()
    for copy in copies[:4]:
        copy.wait()
    cell, owner, share = cell_buf[...], owner_buf[...], share_buf[...]
    for ref in (to_high, to_low):
        put_row(ref, G_LIST, cell.astype(F32))
        put_row(ref, G_LIST + 4, owner.astype(F32))
        put_row(ref, G_LIST + 8, share)
        ref[G_LIST + LIST_ROWS : G_ROWS, :] = jnp.zeros((4, BK), F32)
    row = iota((8, BK), 0)
    sides = jnp.where(row == 0, face_buf[0, 0, 0], jnp.where(row == 1, face_buf[0, 0, 1], 0))
    info[...] = sides.astype(F32)
    pick = jnp.where(iota((CELLS, DMAX), 0) == cell // BK, 1.0, 0.0).astype(BF16)
    mine = iota((64, DMAX), 0)
    copies[4].wait()
    parts = jnp.concatenate(three(block[0][inside].reshape(CELLS, BK)), axis=1)
    found = lax.dot_general(parts, pick, (((0,), (0,)), ((), ())), preferred_element_type=F32)
    found = found[:BK] + found[BK : 2 * BK] + found[2 * BK :]
    inflow = jnp.sum(jnp.where(iota((BK, DMAX), 0) == cell % BK, found, 0.0), axis=0, keepdims=True)
    both = jnp.where(mine == owner, inflow, 0.0) + jnp.where(mine == owner + 32, 1.0, 0.0)
    both = jnp.concatenate([both, jnp.zeros((64, DMAX), F32)], axis=0)
    total = lax.dot_general(
        jnp.ones((8, DMAX), F32),
        both,
        (((1,), (1,)), ((), ())),
        precision=lax.Precision.HIGHEST,
        preferred_element_type=F32,
    )
    for t in range(sums.shape[0] // 8):
        sums[t * 8 : t * 8 + 8, :] = total
    for f in range(5):
        if f == 4:
            copies[8].wait()
            copies[9].wait()
            block[4][inside] = viscosity + k_buf[...] / w_buf[...]
        elif f:
            copies[4 + f].wait()
        flat = lines(block[f])
        n = COLS[f]
        for c in range(n):
            at = (COL_AT[f] + c) * BI
            to_high[at : at + BI, :] = flat[pl.ds(4 * EC + OWN + BJ - n + c, BI, stride=EC), :]
            to_low[at : at + BI, :] = flat[pl.ds(4 * EC + OWN + c, BI, stride=EC), :]


def listed(own, from_low, from_high):
    rows = [
        jnp.concatenate([wide_row(ref, G_LIST + 4 * q) for ref in (own, from_low, from_high)], axis=1)
        for q in range(3)
    ]
    return rows[0].astype(I32), rows[1].astype(I32), rows[2]


def list_load(owner, share, load):
    mine = jnp.where(iota((BK, owner.shape[1]), 0) == owner, 1.0, 0.0)
    given = jnp.dot(load, mine, precision=lax.Precision.HIGHEST, preferred_element_type=F32)
    return given[:1] * share


def spread_rows(cell, given, row, count):
    size = cell.shape[1]
    here = jnp.where(iota((BK, size), 0) == cell % BK, 1.0, 0.0).astype(BF16)
    hit = iota((count, size), 0) == row
    picks = [jnp.where(hit, part.astype(F32), 0.0).astype(BF16) for part in three(given)]
    out = lax.dot_general(
        jnp.concatenate(picks, axis=0), here, (((1,), (1,)), ((), ())), preferred_element_type=F32
    )
    return out[:count] + out[count : 2 * count] + out[2 * count :]


def middle_kernel(*refs):
    (from_low, from_high, own_list, sums, info) = refs[5:10]
    block, (up, down, load) = refs[10:15], refs[15:18]
    for f in range(5):
        flat, m = lines(block[f]), COLS[f]
        for c in range(m):
            at = (COL_AT[f] + c) * BI
            flat[pl.ds(4 * EC + LO + 4 - m + c, BI, stride=EC), :] = from_low[at : at + BI, :]
            flat[pl.ds(4 * EC + HI + c, BI, stride=EC), :] = from_high[at : at + BI, :]
    total = jnp.sum(sums[...], axis=0, keepdims=True)
    filled = pltpu.roll(jnp.broadcast_to(total, (8, BK)), BK - 32, 1)[:1]
    value = thrust * (target_speed - total / jnp.maximum(filled, 1.0))
    value = jnp.broadcast_to(jnp.where(iota((1, BK), 1) < 32, value, 0.0), (8, BK))
    load[...] = value

    cell, owner, share = listed(own_list, from_low, from_high)
    i, j = cell // (BJ * BK), (cell // BK) % BJ
    side = iota(cell.shape, 1) // DMAX
    edge = jnp.where(i < 3, i, jnp.where(i >= BI - 3, i - (BI - 6), -1))
    own_row = jnp.where(edge >= 0, edge * BJ + j, -1)
    corner = jnp.where(i < 2, i, jnp.where(i >= BI - 2, i - (BI - 4), -1))
    first = jnp.where(side == 1, BJ - 2, 0)
    across = j - first
    near = (corner >= 0) & (across >= 0) & (across < 2)
    side_row = jnp.where(near, 6 * BJ + (side - 1) * 8 + corner * 2 + across, -1)
    row = jnp.where(side == 0, own_row, side_row)
    force = spread_rows(cell, list_load(owner, share, value), row, 6 * BJ + 16)

    for f in range(5):
        n = LAYERS[f]
        for q in range(n):
            at = (LAYER_AT[f] + q) * WIDE
            for ref, l in ((up, 4 + BI - n + q), (down, 4 + q)):
                ref[at : at + BJ, :] = block[f][l, OWN : OWN + BJ, :]
                ref[at + BJ : at + BJ + 4, :] = block[f][l, LO : LO + 4, :]
                ref[at + BJ + 4 : at + WIDE, :] = block[f][l, HI : HI + 4, :]
    for q in range(3):
        at = (FORCE_AT + q) * WIDE
        for ref, e, c in ((up, 3 + q, 1 + q), (down, q, q)):
            ref[at : at + BJ, :] = force[e * BJ : (e + 1) * BJ]
            ref[at + BJ : at + WIDE, :] = jnp.zeros((8, BK), F32)
            if (ref is up and q > 0) or (ref is down and q < 2):
                low = 6 * BJ + 2 * c
                ref[at + BJ + 2 : at + BJ + 4, :] = force[low : low + 2]
                ref[at + BJ + 4 : at + BJ + 6, :] = force[low + 8 : low + 10]
    for ref in (up, down):
        ref[S_FACE : S_FACE + 8, :] = info[...]


def images(ref, start, count, low_turned, high_turned, outer=True):
    flat = lines(ref)
    backward = BK - 1 - iota((count, BK), 1)
    for source, target, mask in (
        (LO + 3, LO_IN, low_turned),
        (HI, HI_IN, high_turned),
        (OWN, LO_OUT, low_turned),
        (OWN + BJ - 1, HI_OUT, high_turned),
    )[: 4 if outer else 2]:
        value = flat[pl.ds(start * EC + source, count, stride=EC), :]
        mirror = jnp.take_along_axis(value, backward, axis=1, mode="promise_in_bounds")
        flat[pl.ds(start * EC + target, count, stride=EC), :] = jnp.where(mask, mirror, value)


MID, LEFT, RIGHT = slice(8, 40), slice(7, 39), slice(9, 41)
NEAR, NEAR_LEFT, NEAR_RIGHT = slice(OWN, OWN + BJ), slice(OWN - 1, OWN + BJ - 1), slice(OWN + 1, OWN + BJ + 1)


def below(x, sign):
    return jnp.where(iota(x.shape, 1) == 0, sign * x, pltpu.roll(x, 1, 1))


def above(x):
    return jnp.where(iota(x.shape, 1) == BK - 1, 0.0, pltpu.roll(x, BK - 1, 1))


def star_layer(block, force, star, l):
    e = block[4][l, MID, :]
    share = 1.0 / (1.0 + 3.0 * e)
    half = 0.5 * e
    p = block[3]
    q = p[l, MID, :]
    slope = (
        p[l + 1, MID, :] - p[l - 1, MID, :],
        p[l, RIGHT, :] - p[l, LEFT, :],
        above(q) - below(q, 1.0),
    )
    for c in range(3):
        u = block[c]
        x, a, b = u[l, MID, :], u[l - 1, MID, :], u[l + 1, MID, :]
        around = a + b + u[l, LEFT, :] + u[l, RIGHT, :] + below(x, -1.0) + above(x)
        value = x - 0.125 * (b - a) + half * around - 0.25 * slope[c]
        if c == 0:
            value = value + 0.5 * force[l, MID, :]
        star[c][l, MID, :] = value * share


def sweep_layer(star, sweep, l):
    x = star[2][l, MID, :]
    total = (star[0][l + 1, MID, :] - star[0][l - 1, MID, :]) + (star[1][l, RIGHT, :] - star[1][l, LEFT, :])
    sweep[l, MID, :] = (total + (above(x) - below(x, -1.0))) * (-1.0 / 6.0)


def second_layer(sweep, second, l):
    x = sweep[l, MID, :]
    around = sweep[l - 1, MID, :] + sweep[l + 1, MID, :] + sweep[l, LEFT, :] + sweep[l, RIGHT, :]
    second[l, MID, :] = (around + below(x, 1.0) + above(x)) * (1.0 / 6.0) + x


def out_layer(block, star, second, stage, l, at):
    x = second[l, NEAR, :]
    slope = (
        second[l + 1, NEAR, :] - second[l - 1, NEAR, :],
        second[l, NEAR_RIGHT, :] - second[l, NEAR_LEFT, :],
        above(x) - below(x, 1.0),
    )
    for c in range(3):
        stage[c, at] = star[c][l, NEAR, :] - 0.25 * slope[c]
    stage[3, at] = block[3][l, NEAR, :] + x


def layers(start, stop, step, unroll):
    def run(l, carry):
        step(l)
        return carry

    lax.fori_loop(start, stop, run, 0, unroll=unroll)


def inner_kernel(*refs):
    from_low, from_high, own_list, load, info = refs[5:10]
    block, star, (force, sweep, second) = refs[10:15], refs[15:18], refs[18:21]
    stage = refs[21]
    cell, owner, share = listed(own_list, from_low, from_high)
    given = list_load(owner, share, load[...])
    i, j = cell // (BJ * BK), (cell // BK) % BJ
    own, low, high = (slice(n * DMAX, (n + 1) * DMAX) for n in range(3))
    out = spread_rows(cell[:, own], given[:, own], cell[:, own] // BK, CELLS)
    force[4 : 4 + BI, NEAR, :] = out.reshape(BI, BJ, BK)
    flat = lines(force)
    for part, j0, at in ((low, BJ - 2, LO + 2), (high, 0, HI)):
        across = j[:, part] - j0
        row = jnp.where((across >= 0) & (across < 2), across * BI + i[:, part], -1)
        out = spread_rows(cell[:, part], given[:, part], row, 2 * BI)
        for c in range(2):
            flat[pl.ds(4 * EC + at + c, BI, stride=EC), :] = out[c * BI : (c + 1) * BI]
    low_turned, high_turned = info[0:1, :] > 0.5, info[1:2, :] > 0.5
    a, b = INNER
    for f in range(4):
        images(block[f], 4, BI, low_turned, high_turned)
    layers(a - 3, b + 3, lambda l: star_layer(block, force, star, l), 2)
    images(star[1], a - 3, b - a + 6, low_turned, high_turned)
    layers(a - 2, b + 2, lambda l: sweep_layer(star, sweep, l), 4)
    images(sweep, a - 2, b - a + 4, low_turned, high_turned)
    layers(a - 1, b + 1, lambda l: second_layer(sweep, second, l), 2)
    images(second, a - 1, b - a + 2, low_turned, high_turned, outer=False)
    layers(a, b, lambda l: out_layer(block, star, second, stage, l, l - a), 4)


def outer_kernel(*refs):
    from_up, from_down, info, done = refs[11:15]
    refs = refs[15:]
    block, star, (force, sweep, second) = refs[:5], refs[5:8], refs[8:11]
    vel_out, prs_out, stage, sem = refs[11:]
    a, b = INNER
    inside = slice(a - 4, b - 4)
    copies = [pltpu.make_async_copy(done.at[c], vel_out.at[c, inside], sem.at[8 + c]) for c in range(3)]
    copies.append(pltpu.make_async_copy(done.at[3], prs_out.at[inside], sem.at[11]))
    for copy in copies:
        copy.start()
    place = lax.axis_index("stream")
    first_row = place == 0
    last_row = place == lax.axis_size("stream") - 1
    for f in range(6):
        to, n, base = (block[f], LAYERS[f], LAYER_AT[f]) if f < 5 else (force, 3, FORCE_AT)
        for q in range(n):
            at = (base + q) * WIDE
            for ref, l in ((from_up, 4 - n + q), (from_down, 4 + BI + q)):
                to[l, OWN : OWN + BJ, :] = ref[at : at + BJ, :]
                to[l, LO : LO + 4, :] = ref[at + BJ : at + BJ + 4, :]
                to[l, HI : HI + 4, :] = ref[at + BJ + 4 : at + WIDE, :]

    def both(ref, down, outer=True):
        for start, other in ((down, from_up), (EL - 4 - down, from_down)):
            l = iota((4, BK), 0) + start
            here = (l >= 4) & (l < 4 + BI)
            low = jnp.where(here, info[0:1, :], other[S_FACE : S_FACE + 1, :]) > 0.5
            high = jnp.where(here, info[1:2, :], other[S_FACE + 1 : S_FACE + 2, :]) > 0.5
            images(ref, start, 4, low, high, outer)

    def ends(down, step):
        for l in (*range(down, down + 4), *range(EL - 4 - down, EL - down)):
            step(l)

    @pl.when(first_row)
    def _():
        for f in range(3):
            block[f][3] = jnp.zeros((EC, BK), F32)
        block[3][3] = block[3][4]

    @pl.when(last_row)
    def _():
        for f in range(3):
            block[f][4 + BI] = block[f][3 + BI]
        block[3][4 + BI] = jnp.zeros((EC, BK), F32)

    for f in range(4):
        both(block[f], 0)
    ends(1, lambda l: star_layer(block, force, star, l))

    @pl.when(first_row)
    def _():
        star[0][3] = jnp.zeros((EC, BK), F32)

    @pl.when(last_row)
    def _():
        star[0][4 + BI] = star[0][3 + BI]

    both(star[1], 1)
    ends(2, lambda l: sweep_layer(star, sweep, l))

    @pl.when(first_row)
    def _():
        sweep[3] = sweep[4]

    @pl.when(last_row)
    def _():
        sweep[4 + BI] = jnp.zeros((EC, BK), F32)

    both(sweep, 2)
    ends(3, lambda l: second_layer(sweep, second, l))

    @pl.when(first_row)
    def _():
        second[3] = second[4]

    @pl.when(last_row)
    def _():
        second[4 + BI] = jnp.zeros((EC, BK), F32)

    both(second, 3, outer=False)
    both(second, 4, outer=False)
    for start in (4, b):
        at = 0 if start == 4 else 4
        for q in range(4):
            out_layer(block, star, second, stage, start + q, at + q)
        part, to = slice(at, at + 4), slice(start - 4, start)
        for c in range(3):
            copies.append(pltpu.make_async_copy(stage.at[c, part], vel_out.at[c, to], sem.at[at + c]))
        copies.append(pltpu.make_async_copy(stage.at[3, part], prs_out.at[to], sem.at[at + 3]))
        for copy in copies[at + 4 :]:
            copy.start()
    for copy in copies:
        copy.wait()


def body(velocity, pressure, turb_k, turb_omega, face_code, disc_cells, disc_sector, disc_weight):
    streams, girths = lax.axis_size("stream"), lax.axis_size("girth")
    vmem = pl.BlockSpec(memory_space=pltpu.VMEM)
    hbm = pl.BlockSpec(memory_space=pltpu.HBM)
    params = pltpu.CompilerParams(vmem_limit_bytes=24 * 2**20)

    def struct(*shape):
        return jax.ShapeDtypeStruct(shape, F32)

    block = struct(EL, EC, BK)
    fields = (velocity, pressure, turb_k, turb_omega, disc_cells, disc_sector.reshape(1, DMAX), disc_weight, face_code)
    *exts, sums, to_high, to_low, info = pl.pallas_call(
        head_kernel,
        out_shape=(block,) * 5 + (struct(girths, BK), struct(G_ROWS, BK), struct(G_ROWS, BK), struct(8, BK)),
        in_specs=[hbm] * 8,
        out_specs=(vmem,) * 9,
        scratch_shapes=[
            pltpu.VMEM((BI, BJ, BK), F32),
            pltpu.VMEM((BI, BJ, BK), F32),
            pltpu.VMEM((1, DMAX), I32),
            pltpu.VMEM((1, DMAX), I32),
            pltpu.VMEM((1, DMAX), F32),
            pltpu.SMEM((1, 1, 2), I32),
            pltpu.SemaphoreType.DMA((10,)),
        ],
        compiler_params=params,
        name="head",
    )(*(pltpu.with_memory_space_constraint(x, pltpu.HBM) for x in fields))
    ring = [(g, (g + 1) % girths) for g in range(girths)]
    from_low = lax.ppermute(to_high, "girth", ring)
    from_high = lax.ppermute(to_low, "girth", [(b, a) for a, b in ring])
    sums = lax.all_to_all(sums, "girth", split_axis=0, concat_axis=0, tiled=True)

    *exts, up, down, load = pl.pallas_call(
        middle_kernel,
        out_shape=(block,) * 5 + (struct(S_ROWS, BK), struct(S_ROWS, BK), struct(8, BK)),
        in_specs=[vmem] * 10,
        out_specs=(vmem,) * 8,
        input_output_aliases={n: n for n in range(5)},
        compiler_params=params,
        name="middle",
    )(*exts, from_low, from_high, to_low, sums, info)
    chain = [(s, s + 1) for s in range(streams - 1)]
    from_up = lax.ppermute(up, "stream", chain)
    from_down = lax.ppermute(down, "stream", [(b, a) for a, b in chain])

    outs = (struct(3, BI, BJ, BK), struct(BI, BJ, BK))
    *exts, done = pl.pallas_call(
        inner_kernel,
        out_shape=(block,) * 11 + (struct(4, INNER[1] - INNER[0], BJ, BK),),
        in_specs=[vmem] * 10,
        out_specs=(vmem,) * 12,
        input_output_aliases={n: n for n in range(5)},
        compiler_params=params,
        name="inner",
    )(*exts, from_low, from_high, to_low, load, info)
    return tuple(
        pl.pallas_call(
            outer_kernel,
            out_shape=(block,) * 11 + outs,
            in_specs=[vmem] * 15,
            out_specs=(vmem,) * 11 + (hbm,) * 2,
            input_output_aliases={n: n for n in range(11)},
            scratch_shapes=[pltpu.VMEM((4, 8, BJ, BK), F32), pltpu.SemaphoreType.DMA((12,))],
            compiler_params=params,
            name="outer",
        )(*exts, from_up, from_down, info, done)[11:]
    )


def solution(mesh):
    block = P("stream", "girth", None)
    placed = (P(None, "stream", "girth", None), block, block, block, block, P("stream", "girth"), block, P("stream", "girth"))
    return jax.shard_map(
        body,
        mesh=mesh,
        in_specs=placed,
        out_specs=(P(None, "stream", "girth", None), block),
        check_vma=False,
    )
```

time: 80 us -> 61.2 us (0.77)
  the two profiles are of different devices: /device:TPU:1 before, /device:TPU:6 now
where the time goes in v2:
time: 61.2 us; the launch traced here: 60.7 us
  starting transfers between devices  26.8 us (44%)
  blocking collectives  22.2 us (36%)
  Pallas kernels  11.1 us (18%)
  between operations  0.71 us (1%)
    all_to_all x1, blocking collectives, body(): lax.all_to_all(sums, 'girth', split_axis=0, concat_axis=0, tiled=True)  22.2 us
    ppermute x1, starting transfers between devices, body(): from_high = lax.ppermute(to_low, 'girth', [(b, a) for a, b in ring])  15.9 us
    pallas_call x1, Pallas kernels, body(): pl.pallas_call(inner_kernel, out_shape=(block,) * 11 + (struct(4, INNER[1...  6.16 us
    ppermute x1, starting transfers between devices, body(): from_down = lax.ppermute(down, 'stream', [(b, a) for a, b in chain])  5.44 us
    ppermute x1, starting transfers between devices, body(): from_low = lax.ppermute(to_high, 'girth', ring)  3.48 us
    pallas_call x1, Pallas kernels, body(): pl.pallas_call(head_kernel, out_shape=(block,) * 5 + (struct(girths, BK),...  2.03 us
    ppermute x1, starting transfers between devices, body(): from_up = lax.ppermute(up, 'stream', chain)  1.92 us
    pallas_call x1, Pallas kernels, body(): pl.pallas_call(outer_kernel, out_shape=(block,) * 11 + outs, in_specs=[vm...  1.72 us
  transfers between devices with their start and end apart: 4, of which 0 were waited for; matrix products, arithmetic and copies ran while one was open for 0% of the time, Pallas kernels for 10%

profile of v2, /device:TPU:6, one launch (start us, length us, event | category | flops | bytes accessed | tf_op | source)
XLA Modules:
  0.0 60.7 jit_solution(9877674751038472756)
XLA Ops:
  0.6 2.0 %head.1 = (f32[40,48,128]{2,1,0:T(8,128)S(1)}, f32[40,48,128]{2,1,0:T(8,128)S(1)}, f32[40,48,128]{2,1,0:T(8,128)S(1)}, f32[40,48,128]{2,1,0:T(8,128)S(1)}, f32[4...) custom-call(f32[3,32,16,128]{3,2,1,0:T(8,128)} %vel.1, ...), custom_call_target="tpu_custom_call" | custom-call | tf_op jit(solution)/shard_map/head/pallas_call | solution.py:410
  2.7 3.5 %collective-permute-start = (f32[560,128]{1,0:T(8,128)S(1)}, f32[560,128]{1,0:T(8,128)S(1)}, u32[]{:S(2)}, u32[]{:S(2)}) collective-permute-start(f32[560,128]{1,0:T(8,128)S(1)} %get-tuple-element.38), channel_id=1, source_target_pairs={{0,1},{1,2},{2,3},{3,4},{4,5},{5,6},{6,7},{7,8},{8,9},{9,10},{10,1... | collective-permute-start | bytes 860168 | tf_op jit(solution)/shard_map/ppermute | solution.py:428
  6.2 15.9 %collective-permute-start.1 = (f32[560,128]{1,0:T(8,128)S(1)}, f32[560,128]{1,0:T(8,128)S(1)}, u32[]{:S(2)}, u32[]{:S(2)}) collective-permute-start(f32[560,128]{1,0:T(8,128)S(1)} %get-tuple-element.39.refs_7_), channel_id=1, source_target_pairs={{1,0},{2,1},{3,2},{4,3},{5,4},{6,5},{7,6},{8,7},{9,8},{10,9},{11,1... | collective-permute-start | bytes 860168 | tf_op jit(solution)/shard_map/ppermute | solution.py:429
  22.1 22.2 %all_to_all.11 = f32[32,1,128]{2,1,0:T(1,128)S(1)} all-to-all(f32[32,1,128]{2,1,0:T(1,128)S(1)} %bitcast.6), channel_id=1, replica_groups=mesh['stream'=24,'girth'=32] {'girth'}, dimensions={0} | all-to-all | bytes 32768 | tf_op jit(solution)/shard_map/all_to_all | solution.py:430
  44.3 0.0 collective-permute-done.refs_5_
  44.3 0.0 collective-permute-done.1.refs_6_
  44.3 1.1 %middle.1 = (f32[40,48,128]{2,1,0:T(8,128)S(1)}, f32[40,48,128]{2,1,0:T(8,128)S(1)}, f32[40,48,128]{2,1,0:T(8,128)S(1)}, f32[40,48,128]{2,1,0:T(8,128)S(1)}, f32...) custom-call(f32[40,48,128]{2,1,0:T(8,128)S(1)} %get-tuple-element.33, ...), custom_call_target="tpu_custom_call", output_to_operand_aliasing={{0}: (0, {}), {1}: (1, {}), {2}: (2, {}), {3}: (3, {}), {4}... | custom-call | tf_op jit(solution)/shard_map/middle/pallas_call | solution.py:432
  45.4 1.9 %collective-permute-start.2 = (f32[488,128]{1,0:T(8,128)S(1)}, f32[488,128]{1,0:T(8,128)S(1)}, u32[]{:S(2)}, u32[]{:S(2)}) collective-permute-start(f32[488,128]{1,0:T(8,128)S(1)} %get-tuple-element.59), channel_id=1, source_target_pairs={{0,32},{32,64},{64,96},{96,128},{128,160},{160,192},{192,224},{224... | collective-permute-start | bytes 749576 | tf_op jit(solution)/shard_map/ppermute | solution.py:442
  47.4 5.4 %collective-permute-start.3 = (f32[488,128]{1,0:T(8,128)S(1)}, f32[488,128]{1,0:T(8,128)S(1)}, u32[]{:S(2)}, u32[]{:S(2)}) collective-permute-start(f32[488,128]{1,0:T(8,128)S(1)} %get-tuple-element.60), channel_id=1, source_target_pairs={{32,0},{64,32},{96,64},{128,96},{160,128},{192,160},{224,192},{256... | collective-permute-start | bytes 749576 | tf_op jit(solution)/shard_map/ppermute | solution.py:443
  52.8 6.2 %inner.1 = (f32[40,48,128]{2,1,0:T(8,128)S(1)}, f32[40,48,128]{2,1,0:T(8,128)S(1)}, f32[40,48,128]{2,1,0:T(8,128)S(1)}, f32[40,48,128]{2,1,0:T(8,128)S(1)}, f32[...) custom-call(f32[40,48,128]{2,1,0:T(8,128)S(1)} %get-tuple-element.42, ...), custom_call_target="tpu_custom_call", output_to_operand_aliasing={{0}: (0, {}), {1}: (1, {}), {2}: (2, {}), {3}: (3, {}), {4}... | custom-call | tf_op jit(solution)/shard_map/inner/pallas_call | solution.py:446
  59.0 0.0 collective-permute-done.2.refs_11_
  59.0 0.0 collective-permute-done.3.refs_12_
  59.0 1.7 %outer.1 = (f32[40,48,128]{2,1,0:T(8,128)S(1)}, f32[40,48,128]{2,1,0:T(8,128)S(1)}, f32[40,48,128]{2,1,0:T(8,128)S(1)}, f32[40,48,128]{2,1,0:T(8,128)S(1)}, f32[...) custom-call(f32[40,48,128]{2,1,0:T(8,128)S(1)} %get-tuple-element.48, ...), custom_call_target="tpu_custom_call", output_to_operand_aliasing={{0}: (0, {}), {1}: (1, {}), {2}: (2, {}), {3}: (3, {}), {4}... | custom-call | tf_op jit(solution)/shard_map/outer/pallas_call | solution.py:456
Async XLA Ops:
  2.7 41.6 %collective-permute-start = (f32[560,128]{1,0:T(8,128)S(1)}, f32[560,128]{1,0:T(8,128)S(1)}, u32[]{:S(2)}, u32[]{:S(2)}) collective-permute-start(f32[560,128]{1,0:T(8,128)S(1)} %get-tuple-element.38), channel_id=1, source_target_pairs={{0,1},{1,2},{2,3},{3,4},{4,5},{5,6},{6,7},{7,8},{8,9},{9,10},{10,1... | collective-permute-start | bytes 860168 | tf_op jit(solution)/shard_map/ppermute | solution.py:428
  6.2 38.1 %collective-permute-start.1 = (f32[560,128]{1,0:T(8,128)S(1)}, f32[560,128]{1,0:T(8,128)S(1)}, u32[]{:S(2)}, u32[]{:S(2)}) collective-permute-start(f32[560,128]{1,0:T(8,128)S(1)} %get-tuple-element.39.refs_7_), channel_id=1, source_target_pairs={{1,0},{2,1},{3,2},{4,3},{5,4},{6,5},{7,6},{8,7},{9,8},{10,9},{11,1... | collective-permute-start | bytes 860168 | tf_op jit(solution)/shard_map/ppermute | solution.py:429
  45.4 13.5 %collective-permute-start.2 = (f32[488,128]{1,0:T(8,128)S(1)}, f32[488,128]{1,0:T(8,128)S(1)}, u32[]{:S(2)}, u32[]{:S(2)}) collective-permute-start(f32[488,128]{1,0:T(8,128)S(1)} %get-tuple-element.59), channel_id=1, source_target_pairs={{0,32},{32,64},{64,96},{96,128},{128,160},{160,192},{192,224},{224... | collective-permute-start | bytes 749576 | tf_op jit(solution)/shard_map/ppermute | solution.py:442
  47.4 11.6 %collective-permute-start.3 = (f32[488,128]{1,0:T(8,128)S(1)}, f32[488,128]{1,0:T(8,128)S(1)}, u32[]{:S(2)}, u32[]{:S(2)}) collective-permute-start(f32[488,128]{1,0:T(8,128)S(1)} %get-tuple-element.60), channel_id=1, source_target_pairs={{32,0},{64,32},{96,64},{128,96},{160,128},{192,160},{224,192},{256... | collective-permute-start | bytes 749576 | tf_op jit(solution)/shard_map/ppermute | solution.py:443

commit v3 on v2

--- a/solution.py
+++ b/solution.py
@@ -32,6 +32,16 @@
     return lax.broadcasted_iota(I32, shape, dim)
 
 
+def is_odd(axis):
+    return lax.axis_index(axis) % 2 == 1
+
+
+def by_parity(axis, even, odd):
+    flag = is_odd(axis)
+    pl.when(jnp.logical_not(flag))(even)
+    pl.when(flag)(odd)
+
+
 def three(x):
     a = x.astype(BF16)
     rest = x - a.astype(F32)
@@ -54,7 +64,7 @@
 
 
 def head_kernel(vel, prs, tk, tw, cells, sector, weight, face, *refs):
-    block, (sums, to_high, to_low, info) = refs[:5], refs[5:9]
+    block, (sums, pack_a, pack_b, info) = refs[:5], refs[5:9]
     k_buf, w_buf, cell_buf, owner_buf, share_buf, face_buf, sem = refs[9:]
     inside = (slice(4, 4 + BI), slice(OWN, OWN + BJ))
     pairs = (
@@ -75,7 +85,7 @@
     for copy in copies[:4]:
         copy.wait()
     cell, owner, share = cell_buf[...], owner_buf[...], share_buf[...]
-    for ref in (to_high, to_low):
+    for ref in (pack_a, pack_b):
         put_row(ref, G_LIST, cell.astype(F32))
         put_row(ref, G_LIST + 4, owner.astype(F32))
         put_row(ref, G_LIST + 8, share)
@@ -101,32 +111,33 @@
     )
     for t in range(sums.shape[0] // 8):
         sums[t * 8 : t * 8 + 8, :] = total
-    for f in range(5):
-        if f == 4:
-            copies[8].wait()
-            copies[9].wait()
-            block[4][inside] = viscosity + k_buf[...] / w_buf[...]
-        elif f:
-            copies[4 + f].wait()
-        flat = lines(block[f])
-        n = COLS[f]
-        for c in range(n):
-            at = (COL_AT[f] + c) * BI
-            to_high[at : at + BI, :] = flat[pl.ds(4 * EC + OWN + BJ - n + c, BI, stride=EC), :]
-            to_low[at : at + BI, :] = flat[pl.ds(4 * EC + OWN + c, BI, stride=EC), :]
-
-
-def listed(own, from_low, from_high):
-    rows = [
-        jnp.concatenate([wide_row(ref, G_LIST + 4 * q) for ref in (own, from_low, from_high)], axis=1)
-        for q in range(3)
-    ]
+    for n in (5, 6, 7, 8, 9):
+        copies[n].wait()
+    block[4][inside] = viscosity + k_buf[...] / w_buf[...]
+
+    def pack(to_high, to_low):
+        for f in range(5):
+            flat, n = lines(block[f]), COLS[f]
+            for c in range(n):
+                at = (COL_AT[f] + c) * BI
+                to_high[at : at + BI, :] = flat[pl.ds(4 * EC + OWN + BJ - n + c, BI, stride=EC), :]
+                to_low[at : at + BI, :] = flat[pl.ds(4 * EC + OWN + c, BI, stride=EC), :]
+
+    by_parity("girth", lambda: pack(pack_a, pack_b), lambda: pack(pack_b, pack_a))
+
+
+def listed(own, pair_a, pair_b):
+    flag = is_odd("girth")
+    rows = []
+    for at in (G_LIST, G_LIST + 4, G_LIST + 8):
+        a, b = wide_row(pair_a, at), wide_row(pair_b, at)
+        rows.append(jnp.concatenate([wide_row(own, at), jnp.where(flag, a, b), jnp.where(flag, b, a)], axis=1))
     return rows[0].astype(I32), rows[1].astype(I32), rows[2]
 
 
 def list_load(owner, share, load):
-    mine = jnp.where(iota((BK, owner.shape[1]), 0) == owner, 1.0, 0.0)
-    given = jnp.dot(load, mine, precision=lax.Precision.HIGHEST, preferred_element_type=F32)
+    mine = jnp.where(iota((32, owner.shape[1]), 0) == owner, 1.0, 0.0)
+    given = jnp.dot(load[:, :32], mine, precision=lax.Precision.HIGHEST, preferred_element_type=F32)
     return given[:1] * share
 
 
@@ -142,21 +153,26 @@
 
 
 def middle_kernel(*refs):
-    (from_low, from_high, own_list, sums, info) = refs[5:10]
-    block, (up, down, load) = refs[10:15], refs[15:18]
-    for f in range(5):
-        flat, m = lines(block[f]), COLS[f]
-        for c in range(m):
-            at = (COL_AT[f] + c) * BI
-            flat[pl.ds(4 * EC + LO + 4 - m + c, BI, stride=EC), :] = from_low[at : at + BI, :]
-            flat[pl.ds(4 * EC + HI + c, BI, stride=EC), :] = from_high[at : at + BI, :]
+    (pair_a, pair_b, own_list, sums, info) = refs[5:10]
+    block, (pack_b, pack_a, spots), (force,) = refs[10:15], refs[15:18], refs[18:]
+
+    def fill(from_low, from_high):
+        for f in range(5):
+            flat, m = lines(block[f]), COLS[f]
+            for c in range(m):
+                at = (COL_AT[f] + c) * BI
+                flat[pl.ds(4 * EC + LO + 4 - m + c, BI, stride=EC), :] = from_low[at : at + BI, :]
+                flat[pl.ds(4 * EC + HI + c, BI, stride=EC), :] = from_high[at : at + BI, :]
+
+    by_parity("girth", lambda: fill(pair_b, pair_a), lambda: fill(pair_a, pair_b))
     total = jnp.sum(sums[...], axis=0, keepdims=True)
     filled = pltpu.roll(jnp.broadcast_to(total, (8, BK)), BK - 32, 1)[:1]
     value = thrust * (target_speed - total / jnp.maximum(filled, 1.0))
     value = jnp.broadcast_to(jnp.where(iota((1, BK), 1) < 32, value, 0.0), (8, BK))
-    load[...] = value
-
-    cell, owner, share = listed(own_list, from_low, from_high)
+    cell, owner, share = listed(own_list, pair_a, pair_b)
+    given = list_load(owner, share, value)
+    spots[0:1, :] = cell.astype(F32)
+    spots[1:2, :] = given
     i, j = cell // (BJ * BK), (cell // BK) % BJ
     side = iota(cell.shape, 1) // DMAX
     edge = jnp.where(i < 3, i, jnp.where(i >= BI - 3, i - (BI - 6), -1))
@@ -167,8 +183,15 @@
     near = (corner >= 0) & (across >= 0) & (across < 2)
     side_row = jnp.where(near, 6 * BJ + (side - 1) * 8 + corner * 2 + across, -1)
     row = jnp.where(side == 0, own_row, side_row)
-    force = spread_rows(cell, list_load(owner, share, value), row, 6 * BJ + 16)
-
+    force[...] = spread_rows(cell, given, row, 6 * BJ + 16)
+    by_parity(
+        "stream",
+        lambda: stream_packs(block, force, info, pack_a, pack_b),
+        lambda: stream_packs(block, force, info, pack_b, pack_a),
+    )
+
+
+def stream_packs(block, force, info, up, down):
     for f in range(5):
         n = LAYERS[f]
         for q in range(n):
@@ -270,11 +293,10 @@
 
 
 def inner_kernel(*refs):
-    from_low, from_high, own_list, load, info = refs[5:10]
-    block, star, (force, sweep, second) = refs[10:15], refs[15:18], refs[18:21]
-    stage = refs[21]
-    cell, owner, share = listed(own_list, from_low, from_high)
-    given = list_load(owner, share, load[...])
+    spots, info = refs[5], refs[6].at[S_FACE : S_FACE + 8, :]
+    block, star, (force, sweep, second) = refs[7:12], refs[12:15], refs[15:18]
+    stage = refs[18]
+    cell, given = spots[0:1, :].astype(I32), spots[1:2, :]
     i, j = cell // (BJ * BK), (cell // BK) % BJ
     own, low, high = (slice(n * DMAX, (n + 1) * DMAX) for n in range(3))
     out = spread_rows(cell[:, own], given[:, own], cell[:, own] // BK, CELLS)
@@ -290,17 +312,17 @@
     a, b = INNER
     for f in range(4):
         images(block[f], 4, BI, low_turned, high_turned)
-    layers(a - 3, b + 3, lambda l: star_layer(block, force, star, l), 2)
+    layers(a - 3, b + 3, lambda l: star_layer(block, force, star, l), 15)
     images(star[1], a - 3, b - a + 6, low_turned, high_turned)
-    layers(a - 2, b + 2, lambda l: sweep_layer(star, sweep, l), 4)
+    layers(a - 2, b + 2, lambda l: sweep_layer(star, sweep, l), 28)
     images(sweep, a - 2, b - a + 4, low_turned, high_turned)
-    layers(a - 1, b + 1, lambda l: second_layer(sweep, second, l), 2)
+    layers(a - 1, b + 1, lambda l: second_layer(sweep, second, l), 26)
     images(second, a - 1, b - a + 2, low_turned, high_turned, outer=False)
-    layers(a, b, lambda l: out_layer(block, star, second, stage, l, l - a), 4)
+    layers(a, b, lambda l: out_layer(block, star, second, stage, l, l - a), 8)
 
 
 def outer_kernel(*refs):
-    from_up, from_down, info, done = refs[11:15]
+    pair_a, pair_b, info, done = refs[11:15]
     refs = refs[15:]
     block, star, (force, sweep, second) = refs[:5], refs[5:8], refs[8:11]
     vel_out, prs_out, stage, sem = refs[11:]
@@ -313,21 +335,28 @@
     place = lax.axis_index("stream")
     first_row = place == 0
     last_row = place == lax.axis_size("stream") - 1
-    for f in range(6):
-        to, n, base = (block[f], LAYERS[f], LAYER_AT[f]) if f < 5 else (force, 3, FORCE_AT)
-        for q in range(n):
-            at = (base + q) * WIDE
-            for ref, l in ((from_up, 4 - n + q), (from_down, 4 + BI + q)):
-                to[l, OWN : OWN + BJ, :] = ref[at : at + BJ, :]
-                to[l, LO : LO + 4, :] = ref[at + BJ : at + BJ + 4, :]
-                to[l, HI : HI + 4, :] = ref[at + BJ + 4 : at + WIDE, :]
+
+    def fill(from_up, from_down):
+        for f in range(6):
+            to, n, base = (block[f], LAYERS[f], LAYER_AT[f]) if f < 5 else (force, 3, FORCE_AT)
+            for q in range(n):
+                at = (base + q) * WIDE
+                for ref, l in ((from_up, 4 - n + q), (from_down, 4 + BI + q)):
+                    to[l, OWN : OWN + BJ, :] = ref[at : at + BJ, :]
+                    to[l, LO : LO + 4, :] = ref[at + BJ : at + BJ + 4, :]
+                    to[l, HI : HI + 4, :] = ref[at + BJ + 4 : at + WIDE, :]
+
+    by_parity("stream", lambda: fill(pair_b, pair_a), lambda: fill(pair_a, pair_b))
+    face_a, face_b = pair_a[S_FACE : S_FACE + 8, :], pair_b[S_FACE : S_FACE + 8, :]
+    flag = is_odd("stream")
+    up_face, down_face = jnp.where(flag, face_a, face_b), jnp.where(flag, face_b, face_a)
 
     def both(ref, down, outer=True):
-        for start, other in ((down, from_up), (EL - 4 - down, from_down)):
+        for start, other in ((down, up_face), (EL - 4 - down, down_face)):
             l = iota((4, BK), 0) + start
             here = (l >= 4) & (l < 4 + BI)
-            low = jnp.where(here, info[0:1, :], other[S_FACE : S_FACE + 1, :]) > 0.5
-            high = jnp.where(here, info[1:2, :], other[S_FACE + 1 : S_FACE + 2, :]) > 0.5
+            low = jnp.where(here, info[0:1, :], other[0:1, :]) > 0.5
+            high = jnp.where(here, info[1:2, :], other[1:2, :]) > 0.5
             images(ref, start, 4, low, high, outer)
 
     def ends(down, step):
@@ -407,7 +436,7 @@
 
     block = struct(EL, EC, BK)
     fields = (velocity, pressure, turb_k, turb_omega, disc_cells, disc_sector.reshape(1, DMAX), disc_weight, face_code)
-    *exts, sums, to_high, to_low, info = pl.pallas_call(
+    *exts, sums, pack_a, pack_b, info = pl.pallas_call(
         head_kernel,
         out_shape=(block,) * 5 + (struct(girths, BK), struct(G_ROWS, BK), struct(G_ROWS, BK), struct(8, BK)),
         in_specs=[hbm] * 8,
@@ -424,34 +453,38 @@
         compiler_params=params,
         name="head",
     )(*(pltpu.with_memory_space_constraint(x, pltpu.HBM) for x in fields))
-    ring = [(g, (g + 1) % girths) for g in range(girths)]
-    from_low = lax.ppermute(to_high, "girth", ring)
-    from_high = lax.ppermute(to_low, "girth", [(b, a) for a, b in ring])
+
+    def pairs(size, first, cyclic):
+        ends = [(n, (n + 1) % size) for n in range(first, size, 2) if cyclic or n + 1 < size]
+        return [pair for a, b in ends for pair in ((a, b), (b, a))]
+
+    pair_b = lax.ppermute(pack_b, "girth", pairs(girths, 1, True))
+    pair_a = lax.ppermute(pack_a, "girth", pairs(girths, 0, True))
     sums = lax.all_to_all(sums, "girth", split_axis=0, concat_axis=0, tiled=True)
 
-    *exts, up, down, load = pl.pallas_call(
+    *exts, up_b, up_a, spots = pl.pallas_call(
         middle_kernel,
-        out_shape=(block,) * 5 + (struct(S_ROWS, BK), struct(S_ROWS, BK), struct(8, BK)),
+        out_shape=(block,) * 5 + (struct(S_ROWS, BK), struct(S_ROWS, BK), struct(8, 3 * DMAX)),
         in_specs=[vmem] * 10,
         out_specs=(vmem,) * 8,
         input_output_aliases={n: n for n in range(5)},
+        scratch_shapes=[pltpu.VMEM((6 * BJ + 16, BK), F32)],
         compiler_params=params,
         name="middle",
-    )(*exts, from_low, from_high, to_low, sums, info)
-    chain = [(s, s + 1) for s in range(streams - 1)]
-    from_up = lax.ppermute(up, "stream", chain)
-    from_down = lax.ppermute(down, "stream", [(b, a) for a, b in chain])
+    )(*exts, pair_a, pair_b, pack_a, sums, info)
+    stream_a = lax.ppermute(up_a, "stream", pairs(streams, 0, False))
+    stream_b = lax.ppermute(up_b, "stream", pairs(streams, 1, False))
 
     outs = (struct(3, BI, BJ, BK), struct(BI, BJ, BK))
     *exts, done = pl.pallas_call(
         inner_kernel,
         out_shape=(block,) * 11 + (struct(4, INNER[1] - INNER[0], BJ, BK),),
-        in_specs=[vmem] * 10,
+        in_specs=[vmem] * 7,
         out_specs=(vmem,) * 12,
         input_output_aliases={n: n for n in range(5)},
         compiler_params=params,
         name="inner",
-    )(*exts, from_low, from_high, to_low, load, info)
+    )(*exts, spots, up_a)
     return tuple(
         pl.pallas_call(
             outer_kernel,
@@ -462,7 +495,7 @@
             scratch_shapes=[pltpu.VMEM((4, 8, BJ, BK), F32), pltpu.SemaphoreType.DMA((12,))],
             compiler_params=params,
             name="outer",
-        )(*exts, from_up, from_down, info, done)[11:]
+        )(*exts, stream_a, stream_b, info, done)[11:]
     )
 
 

time: 61.2 us -> 56.5 us (0.923)
  Pallas kernels: 11.1 us -> 7.99 us
  starting transfers between devices: 26.8 us -> 24.2 us
  waiting for transfers between devices: 0.01 us -> 2.19 us
  blocking collectives: 22.2 us -> 21.2 us
    pallas_call x1, Pallas kernels: 6.16 us -> 3.25 us  [body(): pl.pallas_call(inner_kernel, out_shape=(block,) * 11 + (struct(4, INNER[1...]
    ppermute x4, starting transfers between devices: 26.8 us -> 24.2 us  [the longest x1 17.5 us: body(): pair_b = lax.ppermute(pack_b, 'girth', pairs(girths, 1, True))]
    ppermute x4, waiting for transfers between devices: 0.01 us -> 2.19 us  [the longest x1 2.18 us: body(): stream_b = lax.ppermute(up_b, 'stream', pairs(streams, 1, False))]
    all_to_all x1, blocking collectives: 22.2 us -> 21.2 us  [body(): lax.all_to_all(sums, 'girth', split_axis=0, concat_axis=0, tiled=True)]
  transfers between devices with their start and end apart: 4 -> 4, of which waited for: 0 -> 1; matrix products, arithmetic and copies ran while one was open for 0% -> 0% of each run, Pallas kernels for 10% -> 6%
where the time goes in v3:
time: 56.5 us; the launch traced here: 56.2 us
  starting transfers between devices  24.2 us (43%)
  blocking collectives  21.2 us (38%)
  Pallas kernels  7.99 us (14%)
  waiting for transfers between devices  2.19 us (4%)
  between operations  0.69 us (1%)
    all_to_all x1, blocking collectives, body(): lax.all_to_all(sums, 'girth', split_axis=0, concat_axis=0, tiled=True)  21.2 us
    ppermute x1, starting transfers between devices, body(): pair_b = lax.ppermute(pack_b, 'girth', pairs(girths, 1, True))  17.5 us
    pallas_call x1, Pallas kernels, body(): pl.pallas_call(inner_kernel, out_shape=(block,) * 11 + (struct(4, INNER[1...  3.25 us
    ppermute x1, starting transfers between devices, body(): stream_a = lax.ppermute(up_a, 'stream', pairs(streams, 0, False))  2.87 us
    ppermute x1, waiting for transfers between devices, body(): stream_b = lax.ppermute(up_b, 'stream', pairs(streams, 1, False))  2.18 us
    pallas_call x1, Pallas kernels, body(): pl.pallas_call(head_kernel, out_shape=(block,) * 5 + (struct(girths, BK),...  2.02 us
    ppermute x1, starting transfers between devices, body(): pair_a = lax.ppermute(pack_a, 'girth', pairs(girths, 0, True))  1.92 us
    ppermute x1, starting transfers between devices, body(): stream_b = lax.ppermute(up_b, 'stream', pairs(streams, 1, False))  1.92 us
  transfers between devices with their start and end apart: 4, of which 1 were waited for; matrix products, arithmetic and copies ran while one was open for 0% of the time, Pallas kernels for 6%

profile of v3, /device:TPU:6, one launch (start us, length us, event | category | flops | bytes accessed | tf_op | source)
XLA Modules:
  0.0 56.2 jit_solution(12506627656906767930)
XLA Ops:
  0.6 2.0 %head.1 = (f32[40,48,128]{2,1,0:T(8,128)S(1)}, f32[40,48,128]{2,1,0:T(8,128)S(1)}, f32[40,48,128]{2,1,0:T(8,128)S(1)}, f32[40,48,128]{2,1,0:T(8,128)S(1)}, f32[4...) custom-call(f32[3,32,16,128]{3,2,1,0:T(8,128)} %vel.1, ...), custom_call_target="tpu_custom_call" | custom-call | tf_op jit(solution)/shard_map/head/pallas_call | solution.py:439
  2.7 17.5 %collective-permute-start.1 = (f32[560,128]{1,0:T(8,128)S(1)}, f32[560,128]{1,0:T(8,128)S(1)}, u32[]{:S(2)}, u32[]{:S(2)}) collective-permute-start(f32[560,128]{1,0:T(8,128)S(1)} %get-tuple-element.39), channel_id=1, source_target_pairs={{1,2},{2,1},{3,4},{4,3},{5,6},{6,5},{7,8},{8,7},{9,10},{10,9},{11,... | collective-permute-start | bytes 860168 | tf_op jit(solution)/shard_map/ppermute | solution.py:461
  20.1 1.9 %collective-permute-start = (f32[560,128]{1,0:T(8,128)S(1)}, f32[560,128]{1,0:T(8,128)S(1)}, u32[]{:S(2)}, u32[]{:S(2)}) collective-permute-start(f32[560,128]{1,0:T(8,128)S(1)} %get-tuple-element.38.refs_7_), channel_id=1, source_target_pairs={{0,1},{1,0},{2,3},{3,2},{4,5},{5,4},{6,7},{7,6},{8,9},{9,8},{10,11... | collective-permute-start | bytes 860168 | tf_op jit(solution)/shard_map/ppermute | solution.py:462
  22.1 21.2 %all_to_all.11 = f32[32,1,128]{2,1,0:T(1,128)S(1)} all-to-all(f32[32,1,128]{2,1,0:T(1,128)S(1)} %bitcast.6), channel_id=1, replica_groups=mesh['stream'=24,'girth'=32] {'girth'}, dimensions={0} | all-to-all | bytes 32768 | tf_op jit(solution)/shard_map/all_to_all | solution.py:463
  43.2 0.0 collective-permute-done.1.refs_6_
  43.2 0.0 collective-permute-done.refs_5_
  43.2 1.0 %middle.1 = (f32[40,48,128]{2,1,0:T(8,128)S(1)}, f32[40,48,128]{2,1,0:T(8,128)S(1)}, f32[40,48,128]{2,1,0:T(8,128)S(1)}, f32[40,48,128]{2,1,0:T(8,128)S(1)}, f32...) custom-call(f32[40,48,128]{2,1,0:T(8,128)S(1)} %get-tuple-element.33, ...), custom_call_target="tpu_custom_call", output_to_operand_aliasing={{0}: (0, {}), {1}: (1, {}), {2}: (2, {}), {3}: (3, {}), {4}... | custom-call | tf_op jit(solution)/shard_map/middle/pallas_call | solution.py:465
  44.2 1.9 %collective-permute-start.3 = (f32[488,128]{1,0:T(8,128)S(1)}, f32[488,128]{1,0:T(8,128)S(1)}, u32[]{:S(2)}, u32[]{:S(2)}) collective-permute-start(f32[488,128]{1,0:T(8,128)S(1)} %get-tuple-element.60), channel_id=1, source_target_pairs={{32,64},{64,32},{96,128},{128,96},{160,192},{192,160},{224,256},{2... | collective-permute-start | bytes 749576 | tf_op jit(solution)/shard_map/ppermute | solution.py:476
  46.2 2.9 %collective-permute-start.2 = (f32[488,128]{1,0:T(8,128)S(1)}, f32[488,128]{1,0:T(8,128)S(1)}, u32[]{:S(2)}, u32[]{:S(2)}) collective-permute-start(f32[488,128]{1,0:T(8,128)S(1)} %get-tuple-element.48.refs_6_), channel_id=1, source_target_pairs={{0,32},{32,0},{64,96},{96,64},{128,160},{160,128},{192,224},{224,1... | collective-permute-start | bytes 749576 | tf_op jit(solution)/shard_map/ppermute | solution.py:475
  49.0 3.2 %inner.1 = (f32[40,48,128]{2,1,0:T(8,128)S(1)}, f32[40,48,128]{2,1,0:T(8,128)S(1)}, f32[40,48,128]{2,1,0:T(8,128)S(1)}, f32[40,48,128]{2,1,0:T(8,128)S(1)}, f32[...) custom-call(f32[40,48,128]{2,1,0:T(8,128)S(1)} %get-tuple-element.42, ...), custom_call_target="tpu_custom_call", output_to_operand_aliasing={{0}: (0, {}), {1}: (1, {}), {2}: (2, {}), {3}: (3, {}), {4}... | custom-call | tf_op jit(solution)/shard_map/inner/pallas_call | solution.py:479
  52.3 2.2 %collective-permute-done.3.refs_12_ = f32[488,128]{1,0:T(8,128)S(1)} collective-permute-done((f32[488,128]{1,0:T(8,128)S(1)}, f32[488,128]{1,0:T(8,128)S(1)}, u32[]{:S(2)}, u32[]{:S(2)}) %collective-permute-start.3) | collective-permute-done | bytes 249888 | tf_op jit(solution)/shard_map/ppermute | solution.py:476
  54.5 0.0 collective-permute-done.2.refs_11_
  54.5 1.8 %outer.1 = (f32[40,48,128]{2,1,0:T(8,128)S(1)}, f32[40,48,128]{2,1,0:T(8,128)S(1)}, f32[40,48,128]{2,1,0:T(8,128)S(1)}, f32[40,48,128]{2,1,0:T(8,128)S(1)}, f32[...) custom-call(f32[40,48,128]{2,1,0:T(8,128)S(1)} %get-tuple-element.49, ...), custom_call_target="tpu_custom_call", output_to_operand_aliasing={{0}: (0, {}), {1}: (1, {}), {2}: (2, {}), {3}: (3, {}), {4}... | custom-call | tf_op jit(solution)/shard_map/outer/pallas_call | solution.py:489
Async XLA Ops:
  2.7 40.6 %collective-permute-start.1 = (f32[560,128]{1,0:T(8,128)S(1)}, f32[560,128]{1,0:T(8,128)S(1)}, u32[]{:S(2)}, u32[]{:S(2)}) collective-permute-start(f32[560,128]{1,0:T(8,128)S(1)} %get-tuple-element.39), channel_id=1, source_target_pairs={{1,2},{2,1},{3,4},{4,3},{5,6},{6,5},{7,8},{8,7},{9,10},{10,9},{11,... | collective-permute-start | bytes 860168 | tf_op jit(solution)/shard_map/ppermute | solution.py:461
  20.1 23.1 %collective-permute-start = (f32[560,128]{1,0:T(8,128)S(1)}, f32[560,128]{1,0:T(8,128)S(1)}, u32[]{:S(2)}, u32[]{:S(2)}) collective-permute-start(f32[560,128]{1,0:T(8,128)S(1)} %get-tuple-element.38.refs_7_), channel_id=1, source_target_pairs={{0,1},{1,0},{2,3},{3,2},{4,5},{5,4},{6,7},{7,6},{8,9},{9,8},{10,11... | collective-permute-start | bytes 860168 | tf_op jit(solution)/shard_map/ppermute | solution.py:462
  44.2 10.2 %collective-permute-start.3 = (f32[488,128]{1,0:T(8,128)S(1)}, f32[488,128]{1,0:T(8,128)S(1)}, u32[]{:S(2)}, u32[]{:S(2)}) collective-permute-start(f32[488,128]{1,0:T(8,128)S(1)} %get-tuple-element.60), channel_id=1, source_target_pairs={{32,64},{64,32},{96,128},{128,96},{160,192},{192,160},{224,256},{2... | collective-permute-start | bytes 749576 | tf_op jit(solution)/shard_map/ppermute | solution.py:476
  46.2 8.3 %collective-permute-start.2 = (f32[488,128]{1,0:T(8,128)S(1)}, f32[488,128]{1,0:T(8,128)S(1)}, u32[]{:S(2)}, u32[]{:S(2)}) collective-permute-start(f32[488,128]{1,0:T(8,128)S(1)} %get-tuple-element.48.refs_6_), channel_id=1, source_target_pairs={{0,32},{32,0},{64,96},{96,64},{128,160},{160,128},{192,224},{224,1... | collective-permute-start | bytes 749576 | tf_op jit(solution)/shard_map/ppermute | solution.py:475

commit v4 on v3

--- a/solution.py
+++ b/solution.py
@@ -18,9 +18,9 @@
 LIST_ROWS = 12
 G_LIST = 17 * BI
 G_ROWS = G_LIST + 16
-WIDE = BJ + 8
 FORCE_AT = 17
-S_FACE = 20 * WIDE
+S_SIDE = 20 * BJ
+S_FACE = 392
 S_ROWS = S_FACE + 8
 INNER = (8, 32)
 EL, EC = BI + 8, 48
@@ -48,6 +48,19 @@
     b = rest.astype(BF16)
     c = (rest - b.astype(F32)).astype(BF16)
     return a, b, c
+
+
+def side_rows(f):
+    reach = (4, 4, 4, 4, 3, 3)
+    depths = LAYERS + (3,)
+    at = S_SIDE
+    for g in range(f + 1):
+        found = []
+        for d in range(1, depths[g] + 1):
+            width = reach[g] - d
+            found.append((d, at, width))
+            at += 2 * width
+    return found
 
 
 def wide_row(ref, at):
@@ -111,19 +124,20 @@
     )
     for t in range(sums.shape[0] // 8):
         sums[t * 8 : t * 8 + 8, :] = total
-    for n in (5, 6, 7, 8, 9):
-        copies[n].wait()
-    block[4][inside] = viscosity + k_buf[...] / w_buf[...]
-
-    def pack(to_high, to_low):
-        for f in range(5):
+    def pack(to_high, to_low, fields):
+        for f in fields:
             flat, n = lines(block[f]), COLS[f]
             for c in range(n):
                 at = (COL_AT[f] + c) * BI
                 to_high[at : at + BI, :] = flat[pl.ds(4 * EC + OWN + BJ - n + c, BI, stride=EC), :]
                 to_low[at : at + BI, :] = flat[pl.ds(4 * EC + OWN + c, BI, stride=EC), :]
 
-    by_parity("girth", lambda: pack(pack_a, pack_b), lambda: pack(pack_b, pack_a))
+    for waited, fields in (((5, 6, 7), range(4)), ((8, 9), (4,))):
+        for n in waited:
+            copies[n].wait()
+        if 4 in fields:
+            block[4][inside] = viscosity + k_buf[...] / w_buf[...]
+        by_parity("girth", lambda: pack(pack_a, pack_b, fields), lambda: pack(pack_b, pack_a, fields))
 
 
 def listed(own, pair_a, pair_b):
@@ -195,20 +209,24 @@
     for f in range(5):
         n = LAYERS[f]
         for q in range(n):
-            at = (LAYER_AT[f] + q) * WIDE
-            for ref, l in ((up, 4 + BI - n + q), (down, 4 + q)):
-                ref[at : at + BJ, :] = block[f][l, OWN : OWN + BJ, :]
-                ref[at + BJ : at + BJ + 4, :] = block[f][l, LO : LO + 4, :]
-                ref[at + BJ + 4 : at + WIDE, :] = block[f][l, HI : HI + 4, :]
+            at = (LAYER_AT[f] + q) * BJ
+            up[at : at + BJ, :] = block[f][4 + BI - n + q, OWN : OWN + BJ, :]
+            down[at : at + BJ, :] = block[f][4 + q, OWN : OWN + BJ, :]
+        for d, at, width in side_rows(f):
+            if width:
+                for ref, l in ((up, 4 + BI - d), (down, 3 + d)):
+                    ref[at : at + width, :] = block[f][l, LO + 4 - width : LO + 4, :]
+                    ref[at + width : at + 2 * width, :] = block[f][l, HI : HI + width, :]
     for q in range(3):
-        at = (FORCE_AT + q) * WIDE
-        for ref, e, c in ((up, 3 + q, 1 + q), (down, q, q)):
-            ref[at : at + BJ, :] = force[e * BJ : (e + 1) * BJ]
-            ref[at + BJ : at + WIDE, :] = jnp.zeros((8, BK), F32)
-            if (ref is up and q > 0) or (ref is down and q < 2):
+        at = (FORCE_AT + q) * BJ
+        up[at : at + BJ, :] = force[(3 + q) * BJ : (4 + q) * BJ, :]
+        down[at : at + BJ, :] = force[q * BJ : (q + 1) * BJ, :]
+    for d, at, width in side_rows(5):
+        if width:
+            for ref, c in ((up, 4 - d), (down, d - 1)):
                 low = 6 * BJ + 2 * c
-                ref[at + BJ + 2 : at + BJ + 4, :] = force[low : low + 2]
-                ref[at + BJ + 4 : at + BJ + 6, :] = force[low + 8 : low + 10]
+                ref[at : at + width, :] = force[low + 2 - width : low + 2, :]
+                ref[at + width : at + 2 * width, :] = force[low + 8 : low + 8 + width, :]
     for ref in (up, down):
         ref[S_FACE : S_FACE + 8, :] = info[...]
 
@@ -340,11 +358,14 @@
         for f in range(6):
             to, n, base = (block[f], LAYERS[f], LAYER_AT[f]) if f < 5 else (force, 3, FORCE_AT)
             for q in range(n):
-                at = (base + q) * WIDE
-                for ref, l in ((from_up, 4 - n + q), (from_down, 4 + BI + q)):
-                    to[l, OWN : OWN + BJ, :] = ref[at : at + BJ, :]
-                    to[l, LO : LO + 4, :] = ref[at + BJ : at + BJ + 4, :]
-                    to[l, HI : HI + 4, :] = ref[at + BJ + 4 : at + WIDE, :]
+                at = (base + q) * BJ
+                to[4 - n + q, OWN : OWN + BJ, :] = from_up[at : at + BJ, :]
+                to[4 + BI + q, OWN : OWN + BJ, :] = from_down[at : at + BJ, :]
+            for d, at, width in side_rows(f):
+                if width:
+                    for ref, l in ((from_up, 4 - d), (from_down, 3 + BI + d)):
+                        to[l, LO + 4 - width : LO + 4, :] = ref[at : at + width, :]
+                        to[l, HI : HI + width, :] = ref[at + width : at + 2 * width, :]
 
     by_parity("stream", lambda: fill(pair_b, pair_a), lambda: fill(pair_a, pair_b))
     face_a, face_b = pair_a[S_FACE : S_FACE + 8, :], pair_b[S_FACE : S_FACE + 8, :]
@@ -363,53 +384,26 @@
         for l in (*range(down, down + 4), *range(EL - 4 - down, EL - down)):
             step(l)
 
-    @pl.when(first_row)
-    def _():
-        for f in range(3):
-            block[f][3] = jnp.zeros((EC, BK), F32)
-        block[3][3] = block[3][4]
-
-    @pl.when(last_row)
-    def _():
-        for f in range(3):
-            block[f][4 + BI] = block[f][3 + BI]
-        block[3][4 + BI] = jnp.zeros((EC, BK), F32)
-
+    def edges(ref, low, high):
+        ref[3, MID, :] = jnp.where(first_row, low, ref[3, MID, :])
+        ref[4 + BI, MID, :] = jnp.where(last_row, high, ref[4 + BI, MID, :])
+
+    for ref in block[:3]:
+        edges(ref, 0.0, ref[3 + BI, MID, :])
+    edges(block[3], block[3][4, MID, :], 0.0)
     for f in range(4):
         both(block[f], 0)
     ends(1, lambda l: star_layer(block, force, star, l))
 
-    @pl.when(first_row)
-    def _():
-        star[0][3] = jnp.zeros((EC, BK), F32)
-
-    @pl.when(last_row)
-    def _():
-        star[0][4 + BI] = star[0][3 + BI]
-
+    edges(star[0], 0.0, star[0][3 + BI, MID, :])
     both(star[1], 1)
     ends(2, lambda l: sweep_layer(star, sweep, l))
 
-    @pl.when(first_row)
-    def _():
-        sweep[3] = sweep[4]
-
-    @pl.when(last_row)
-    def _():
-        sweep[4 + BI] = jnp.zeros((EC, BK), F32)
-
+    edges(sweep, sweep[4, MID, :], 0.0)
     both(sweep, 2)
     ends(3, lambda l: second_layer(sweep, second, l))
 
-    @pl.when(first_row)
-    def _():
-        second[3] = second[4]
-
-    @pl.when(last_row)
-    def _():
-        second[4 + BI] = jnp.zeros((EC, BK), F32)
-
-    both(second, 3, outer=False)
+    edges(second, second[4, MID, :], 0.0)
     both(second, 4, outer=False)
     for start in (4, b):
         at = 0 if start == 4 else 4

time: 56.5 us -> 55.5 us (0.982)
  waiting for transfers between devices: 2.19 us -> 1.25 us
    ppermute x1, waiting for transfers between devices: 2.18 us -> 1.25 us  [body(): stream_b = lax.ppermute(up_b, 'stream', pairs(streams, 1, False))]
where the time goes in v4:
time: 55.5 us; the launch traced here: 55.2 us
  starting transfers between devices  24.2 us (44%)
  blocking collectives  21.2 us (38%)
  Pallas kernels  7.94 us (14%)
  waiting for transfers between devices  1.25 us (2%)
  between operations  0.69 us (1%)
    all_to_all x1, blocking collectives, body(): lax.all_to_all(sums, 'girth', split_axis=0, concat_axis=0, tiled=True)  21.2 us
    ppermute x1, starting transfers between devices, body(): pair_b = lax.ppermute(pack_b, 'girth', pairs(girths, 1, True))  17.5 us
    pallas_call x1, Pallas kernels, body(): pl.pallas_call(inner_kernel, out_shape=(block,) * 11 + (struct(4, INNER[1...  3.21 us
    ppermute x1, starting transfers between devices, body(): stream_a = lax.ppermute(up_a, 'stream', pairs(streams, 0, False))  2.87 us
    pallas_call x1, Pallas kernels, body(): pl.pallas_call(head_kernel, out_shape=(block,) * 5 + (struct(girths, BK),...  2.03 us
    ppermute x1, starting transfers between devices, body(): pair_a = lax.ppermute(pack_a, 'girth', pairs(girths, 0, True))  1.92 us
    ppermute x1, starting transfers between devices, body(): stream_b = lax.ppermute(up_b, 'stream', pairs(streams, 1, False))  1.92 us
    pallas_call x1, Pallas kernels, body(): pl.pallas_call(outer_kernel, out_shape=(block,) * 11 + outs, in_specs=[vm...  1.73 us
  transfers between devices with their start and end apart: 4, of which 1 were waited for; matrix products, arithmetic and copies ran while one was open for 0% of the time, Pallas kernels for 6%

profile of v4, /device:TPU:6, one launch (start us, length us, event | category | flops | bytes accessed | tf_op | source)
XLA Modules:
  0.0 55.2 jit_solution(987900849927552768)
XLA Ops:
  0.6 2.0 %head.1 = (f32[40,48,128]{2,1,0:T(8,128)S(1)}, f32[40,48,128]{2,1,0:T(8,128)S(1)}, f32[40,48,128]{2,1,0:T(8,128)S(1)}, f32[40,48,128]{2,1,0:T(8,128)S(1)}, f32[4...) custom-call(f32[3,32,16,128]{3,2,1,0:T(8,128)} %vel.1, ...), custom_call_target="tpu_custom_call" | custom-call | tf_op jit(solution)/shard_map/head/pallas_call | solution.py:433
  2.7 17.5 %collective-permute-start.1 = (f32[560,128]{1,0:T(8,128)S(1)}, f32[560,128]{1,0:T(8,128)S(1)}, u32[]{:S(2)}, u32[]{:S(2)}) collective-permute-start(f32[560,128]{1,0:T(8,128)S(1)} %get-tuple-element.39), channel_id=1, source_target_pairs={{1,2},{2,1},{3,4},{4,3},{5,6},{6,5},{7,8},{8,7},{9,10},{10,9},{11,... | collective-permute-start | bytes 860168 | tf_op jit(solution)/shard_map/ppermute | solution.py:455
  20.1 1.9 %collective-permute-start = (f32[560,128]{1,0:T(8,128)S(1)}, f32[560,128]{1,0:T(8,128)S(1)}, u32[]{:S(2)}, u32[]{:S(2)}) collective-permute-start(f32[560,128]{1,0:T(8,128)S(1)} %get-tuple-element.38.refs_7_), channel_id=1, source_target_pairs={{0,1},{1,0},{2,3},{3,2},{4,5},{5,4},{6,7},{7,6},{8,9},{9,8},{10,11... | collective-permute-start | bytes 860168 | tf_op jit(solution)/shard_map/ppermute | solution.py:456
  22.1 21.2 %all_to_all.11 = f32[32,1,128]{2,1,0:T(1,128)S(1)} all-to-all(f32[32,1,128]{2,1,0:T(1,128)S(1)} %bitcast.6), channel_id=1, replica_groups=mesh['stream'=24,'girth'=32] {'girth'}, dimensions={0} | all-to-all | bytes 32768 | tf_op jit(solution)/shard_map/all_to_all | solution.py:457
  43.2 0.0 collective-permute-done.1.refs_6_
  43.3 0.0 collective-permute-done.refs_5_
  43.3 1.0 %middle.1 = (f32[40,48,128]{2,1,0:T(8,128)S(1)}, f32[40,48,128]{2,1,0:T(8,128)S(1)}, f32[40,48,128]{2,1,0:T(8,128)S(1)}, f32[40,48,128]{2,1,0:T(8,128)S(1)}, f32...) custom-call(f32[40,48,128]{2,1,0:T(8,128)S(1)} %get-tuple-element.33, ...), custom_call_target="tpu_custom_call", output_to_operand_aliasing={{0}: (0, {}), {1}: (1, {}), {2}: (2, {}), {3}: (3, {}), {4}... | custom-call | tf_op jit(solution)/shard_map/middle/pallas_call | solution.py:459
  44.2 1.9 %collective-permute-start.3 = (f32[400,128]{1,0:T(8,128)S(1)}, f32[400,128]{1,0:T(8,128)S(1)}, u32[]{:S(2)}, u32[]{:S(2)}) collective-permute-start(f32[400,128]{1,0:T(8,128)S(1)} %get-tuple-element.60), channel_id=1, source_target_pairs={{32,64},{64,32},{96,128},{128,96},{160,192},{192,160},{224,256},{2... | collective-permute-start | bytes 614408 | tf_op jit(solution)/shard_map/ppermute | solution.py:470
  46.2 2.9 %collective-permute-start.2 = (f32[400,128]{1,0:T(8,128)S(1)}, f32[400,128]{1,0:T(8,128)S(1)}, u32[]{:S(2)}, u32[]{:S(2)}) collective-permute-start(f32[400,128]{1,0:T(8,128)S(1)} %get-tuple-element.48.refs_6_), channel_id=1, source_target_pairs={{0,32},{32,0},{64,96},{96,64},{128,160},{160,128},{192,224},{224,1... | collective-permute-start | bytes 614408 | tf_op jit(solution)/shard_map/ppermute | solution.py:469
  49.0 3.2 %inner.1 = (f32[40,48,128]{2,1,0:T(8,128)S(1)}, f32[40,48,128]{2,1,0:T(8,128)S(1)}, f32[40,48,128]{2,1,0:T(8,128)S(1)}, f32[40,48,128]{2,1,0:T(8,128)S(1)}, f32[...) custom-call(f32[40,48,128]{2,1,0:T(8,128)S(1)} %get-tuple-element.42, ...), custom_call_target="tpu_custom_call", output_to_operand_aliasing={{0}: (0, {}), {1}: (1, {}), {2}: (2, {}), {3}: (3, {}), {4}... | custom-call | tf_op jit(solution)/shard_map/inner/pallas_call | solution.py:473
  52.3 1.2 %collective-permute-done.3.refs_12_ = f32[400,128]{1,0:T(8,128)S(1)} collective-permute-done((f32[400,128]{1,0:T(8,128)S(1)}, f32[400,128]{1,0:T(8,128)S(1)}, u32[]{:S(2)}, u32[]{:S(2)}) %collective-permute-start.3) | collective-permute-done | bytes 204832 | tf_op jit(solution)/shard_map/ppermute | solution.py:470
  53.5 0.0 collective-permute-done.2.refs_11_
  53.5 1.7 %outer.1 = (f32[40,48,128]{2,1,0:T(8,128)S(1)}, f32[40,48,128]{2,1,0:T(8,128)S(1)}, f32[40,48,128]{2,1,0:T(8,128)S(1)}, f32[40,48,128]{2,1,0:T(8,128)S(1)}, f32[...) custom-call(f32[40,48,128]{2,1,0:T(8,128)S(1)} %get-tuple-element.49, ...), custom_call_target="tpu_custom_call", output_to_operand_aliasing={{0}: (0, {}), {1}: (1, {}), {2}: (2, {}), {3}: (3, {}), {4}... | custom-call | tf_op jit(solution)/shard_map/outer/pallas_call | solution.py:483
Async XLA Ops:
  2.7 40.6 %collective-permute-start.1 = (f32[560,128]{1,0:T(8,128)S(1)}, f32[560,128]{1,0:T(8,128)S(1)}, u32[]{:S(2)}, u32[]{:S(2)}) collective-permute-start(f32[560,128]{1,0:T(8,128)S(1)} %get-tuple-element.39), channel_id=1, source_target_pairs={{1,2},{2,1},{3,4},{4,3},{5,6},{6,5},{7,8},{8,7},{9,10},{10,9},{11,... | collective-permute-start | bytes 860168 | tf_op jit(solution)/shard_map/ppermute | solution.py:455
  20.1 23.1 %collective-permute-start = (f32[560,128]{1,0:T(8,128)S(1)}, f32[560,128]{1,0:T(8,128)S(1)}, u32[]{:S(2)}, u32[]{:S(2)}) collective-permute-start(f32[560,128]{1,0:T(8,128)S(1)} %get-tuple-element.38.refs_7_), channel_id=1, source_target_pairs={{0,1},{1,0},{2,3},{3,2},{4,5},{5,4},{6,7},{7,6},{8,9},{9,8},{10,11... | collective-permute-start | bytes 860168 | tf_op jit(solution)/shard_map/ppermute | solution.py:456
  44.2 9.3 %collective-permute-start.3 = (f32[400,128]{1,0:T(8,128)S(1)}, f32[400,128]{1,0:T(8,128)S(1)}, u32[]{:S(2)}, u32[]{:S(2)}) collective-permute-start(f32[400,128]{1,0:T(8,128)S(1)} %get-tuple-element.60), channel_id=1, source_target_pairs={{32,64},{64,32},{96,128},{128,96},{160,192},{192,160},{224,256},{2... | collective-permute-start | bytes 614408 | tf_op jit(solution)/shard_map/ppermute | solution.py:470
  46.2 7.3 %collective-permute-start.2 = (f32[400,128]{1,0:T(8,128)S(1)}, f32[400,128]{1,0:T(8,128)S(1)}, u32[]{:S(2)}, u32[]{:S(2)}) collective-permute-start(f32[400,128]{1,0:T(8,128)S(1)} %get-tuple-element.48.refs_6_), channel_id=1, source_target_pairs={{0,32},{32,0},{64,96},{96,64},{128,160},{160,128},{192,224},{224,1... | collective-permute-start | bytes 614408 | tf_op jit(solution)/shard_map/ppermute | solution.py:469

commit v5 on v4

--- a/solution.py
+++ b/solution.py
@@ -170,15 +170,14 @@
     (pair_a, pair_b, own_list, sums, info) = refs[5:10]
     block, (pack_b, pack_a, spots), (force,) = refs[10:15], refs[15:18], refs[18:]
 
-    def fill(from_low, from_high):
-        for f in range(5):
-            flat, m = lines(block[f]), COLS[f]
-            for c in range(m):
-                at = (COL_AT[f] + c) * BI
-                flat[pl.ds(4 * EC + LO + 4 - m + c, BI, stride=EC), :] = from_low[at : at + BI, :]
-                flat[pl.ds(4 * EC + HI + c, BI, stride=EC), :] = from_high[at : at + BI, :]
-
-    by_parity("girth", lambda: fill(pair_b, pair_a), lambda: fill(pair_a, pair_b))
+    flag = is_odd("girth")
+    for f in range(5):
+        flat, m = lines(block[f]), COLS[f]
+        for c in range(m):
+            at = (COL_AT[f] + c) * BI
+            a, b = pair_a[at : at + BI, :], pair_b[at : at + BI, :]
+            flat[pl.ds(4 * EC + LO + 4 - m + c, BI, stride=EC), :] = jnp.where(flag, a, b)
+            flat[pl.ds(4 * EC + HI + c, BI, stride=EC), :] = jnp.where(flag, b, a)
     total = jnp.sum(sums[...], axis=0, keepdims=True)
     filled = pltpu.roll(jnp.broadcast_to(total, (8, BK)), BK - 32, 1)[:1]
     value = thrust * (target_speed - total / jnp.maximum(filled, 1.0))
@@ -354,22 +353,25 @@
     first_row = place == 0
     last_row = place == lax.axis_size("stream") - 1
 
-    def fill(from_up, from_down):
-        for f in range(6):
-            to, n, base = (block[f], LAYERS[f], LAYER_AT[f]) if f < 5 else (force, 3, FORCE_AT)
-            for q in range(n):
-                at = (base + q) * BJ
-                to[4 - n + q, OWN : OWN + BJ, :] = from_up[at : at + BJ, :]
-                to[4 + BI + q, OWN : OWN + BJ, :] = from_down[at : at + BJ, :]
-            for d, at, width in side_rows(f):
-                if width:
-                    for ref, l in ((from_up, 4 - d), (from_down, 3 + BI + d)):
-                        to[l, LO + 4 - width : LO + 4, :] = ref[at : at + width, :]
-                        to[l, HI : HI + width, :] = ref[at + width : at + 2 * width, :]
-
-    by_parity("stream", lambda: fill(pair_b, pair_a), lambda: fill(pair_a, pair_b))
+    flag = is_odd("stream")
+
+    def arrived(at, count):
+        a, b = pair_a[at : at + count, :], pair_b[at : at + count, :]
+        return jnp.where(flag, a, b), jnp.where(flag, b, a)
+
+    for f in range(6):
+        to, n, base = (block[f], LAYERS[f], LAYER_AT[f]) if f < 5 else (force, 3, FORCE_AT)
+        for q in range(n):
+            up, down = arrived((base + q) * BJ, BJ)
+            to[4 - n + q, OWN : OWN + BJ, :] = up
+            to[4 + BI + q, OWN : OWN + BJ, :] = down
+        for d, at, width in side_rows(f):
+            if width:
+                for side, start in ((LO + 4 - width, at), (HI, at + width)):
+                    up, down = arrived(start, width)
+                    to[4 - d, side : side + width, :] = up
+                    to[3 + BI + d, side : side + width, :] = down
     face_a, face_b = pair_a[S_FACE : S_FACE + 8, :], pair_b[S_FACE : S_FACE + 8, :]
-    flag = is_odd("stream")
     up_face, down_face = jnp.where(flag, face_a, face_b), jnp.where(flag, face_b, face_a)
 
     def both(ref, down, outer=True):

time: 55.5 us -> 55.4 us (level)
  no operation moved by 1% of the time
where the time goes in v5:
time: 55.4 us; the launch traced here: 55.1 us
  starting transfers between devices  24.2 us (44%)
  blocking collectives  21.2 us (38%)
  Pallas kernels  7.85 us (14%)
  waiting for transfers between devices  1.24 us (2%)
  between operations  0.69 us (1%)
    all_to_all x1, blocking collectives, body(): lax.all_to_all(sums, 'girth', split_axis=0, concat_axis=0, tiled=True)  21.2 us
    ppermute x1, starting transfers between devices, body(): pair_b = lax.ppermute(pack_b, 'girth', pairs(girths, 1, True))  17.5 us
    pallas_call x1, Pallas kernels, body(): pl.pallas_call(inner_kernel, out_shape=(block,) * 11 + (struct(4, INNER[1...  3.22 us
    ppermute x1, starting transfers between devices, body(): stream_a = lax.ppermute(up_a, 'stream', pairs(streams, 0, False))  2.87 us
    pallas_call x1, Pallas kernels, body(): pl.pallas_call(head_kernel, out_shape=(block,) * 5 + (struct(girths, BK),...  2.03 us
    ppermute x1, starting transfers between devices, body(): stream_b = lax.ppermute(up_b, 'stream', pairs(streams, 1, False))  1.92 us
    ppermute x1, starting transfers between devices, body(): pair_a = lax.ppermute(pack_a, 'girth', pairs(girths, 0, True))  1.92 us
    pallas_call x1, Pallas kernels, body(): pl.pallas_call(outer_kernel, out_shape=(block,) * 11 + outs, in_specs=[vm...  1.71 us
  transfers between devices with their start and end apart: 4, of which 1 were waited for; matrix products, arithmetic and copies ran while one was open for 0% of the time, Pallas kernels for 6%

profile of v5, /device:TPU:6, one launch (start us, length us, event | category | flops | bytes accessed | tf_op | source)
XLA Modules:
  0.0 55.1 jit_solution(17267093074779313614)
XLA Ops:
  0.6 2.0 %head.1 = (f32[40,48,128]{2,1,0:T(8,128)S(1)}, f32[40,48,128]{2,1,0:T(8,128)S(1)}, f32[40,48,128]{2,1,0:T(8,128)S(1)}, f32[40,48,128]{2,1,0:T(8,128)S(1)}, f32[4...) custom-call(f32[3,32,16,128]{3,2,1,0:T(8,128)} %vel.1, ...), custom_call_target="tpu_custom_call" | custom-call | tf_op jit(solution)/shard_map/head/pallas_call | solution.py:435
  2.7 17.5 %collective-permute-start.1 = (f32[560,128]{1,0:T(8,128)S(1)}, f32[560,128]{1,0:T(8,128)S(1)}, u32[]{:S(2)}, u32[]{:S(2)}) collective-permute-start(f32[560,128]{1,0:T(8,128)S(1)} %get-tuple-element.39), channel_id=1, source_target_pairs={{1,2},{2,1},{3,4},{4,3},{5,6},{6,5},{7,8},{8,7},{9,10},{10,9},{11,... | collective-permute-start | bytes 860168 | tf_op jit(solution)/shard_map/ppermute | solution.py:457
  20.1 1.9 %collective-permute-start = (f32[560,128]{1,0:T(8,128)S(1)}, f32[560,128]{1,0:T(8,128)S(1)}, u32[]{:S(2)}, u32[]{:S(2)}) collective-permute-start(f32[560,128]{1,0:T(8,128)S(1)} %get-tuple-element.38.refs_7_), channel_id=1, source_target_pairs={{0,1},{1,0},{2,3},{3,2},{4,5},{5,4},{6,7},{7,6},{8,9},{9,8},{10,11... | collective-permute-start | bytes 860168 | tf_op jit(solution)/shard_map/ppermute | solution.py:458
  22.1 21.2 %all_to_all.11 = f32[32,1,128]{2,1,0:T(1,128)S(1)} all-to-all(f32[32,1,128]{2,1,0:T(1,128)S(1)} %bitcast.6), channel_id=1, replica_groups=mesh['stream'=24,'girth'=32] {'girth'}, dimensions={0} | all-to-all | bytes 32768 | tf_op jit(solution)/shard_map/all_to_all | solution.py:459
  43.2 0.0 collective-permute-done.1.refs_6_
  43.3 0.0 collective-permute-done.refs_5_
  43.3 0.9 %middle.1 = (f32[40,48,128]{2,1,0:T(8,128)S(1)}, f32[40,48,128]{2,1,0:T(8,128)S(1)}, f32[40,48,128]{2,1,0:T(8,128)S(1)}, f32[40,48,128]{2,1,0:T(8,128)S(1)}, f32...) custom-call(f32[40,48,128]{2,1,0:T(8,128)S(1)} %get-tuple-element.33, ...), custom_call_target="tpu_custom_call", output_to_operand_aliasing={{0}: (0, {}), {1}: (1, {}), {2}: (2, {}), {3}: (3, {}), {4}... | custom-call | tf_op jit(solution)/shard_map/middle/pallas_call | solution.py:461
  44.1 1.9 %collective-permute-start.3 = (f32[400,128]{1,0:T(8,128)S(1)}, f32[400,128]{1,0:T(8,128)S(1)}, u32[]{:S(2)}, u32[]{:S(2)}) collective-permute-start(f32[400,128]{1,0:T(8,128)S(1)} %get-tuple-element.60), channel_id=1, source_target_pairs={{32,64},{64,32},{96,128},{128,96},{160,192},{192,160},{224,256},{2... | collective-permute-start | bytes 614408 | tf_op jit(solution)/shard_map/ppermute | solution.py:472
  46.1 2.9 %collective-permute-start.2 = (f32[400,128]{1,0:T(8,128)S(1)}, f32[400,128]{1,0:T(8,128)S(1)}, u32[]{:S(2)}, u32[]{:S(2)}) collective-permute-start(f32[400,128]{1,0:T(8,128)S(1)} %get-tuple-element.48.refs_6_), channel_id=1, source_target_pairs={{0,32},{32,0},{64,96},{96,64},{128,160},{160,128},{192,224},{224,1... | collective-permute-start | bytes 614408 | tf_op jit(solution)/shard_map/ppermute | solution.py:471
  49.0 3.2 %inner.1 = (f32[40,48,128]{2,1,0:T(8,128)S(1)}, f32[40,48,128]{2,1,0:T(8,128)S(1)}, f32[40,48,128]{2,1,0:T(8,128)S(1)}, f32[40,48,128]{2,1,0:T(8,128)S(1)}, f32[...) custom-call(f32[40,48,128]{2,1,0:T(8,128)S(1)} %get-tuple-element.42, ...), custom_call_target="tpu_custom_call", output_to_operand_aliasing={{0}: (0, {}), {1}: (1, {}), {2}: (2, {}), {3}: (3, {}), {4}... | custom-call | tf_op jit(solution)/shard_map/inner/pallas_call | solution.py:475
  52.2 1.2 %collective-permute-done.3.refs_12_ = f32[400,128]{1,0:T(8,128)S(1)} collective-permute-done((f32[400,128]{1,0:T(8,128)S(1)}, f32[400,128]{1,0:T(8,128)S(1)}, u32[]{:S(2)}, u32[]{:S(2)}) %collective-permute-start.3) | collective-permute-done | bytes 204832 | tf_op jit(solution)/shard_map/ppermute | solution.py:472
  53.4 0.0 collective-permute-done.2.refs_11_
  53.4 1.7 %outer.1 = (f32[40,48,128]{2,1,0:T(8,128)S(1)}, f32[40,48,128]{2,1,0:T(8,128)S(1)}, f32[40,48,128]{2,1,0:T(8,128)S(1)}, f32[40,48,128]{2,1,0:T(8,128)S(1)}, f32[...) custom-call(f32[40,48,128]{2,1,0:T(8,128)S(1)} %get-tuple-element.49, ...), custom_call_target="tpu_custom_call", output_to_operand_aliasing={{0}: (0, {}), {1}: (1, {}), {2}: (2, {}), {3}: (3, {}), {4}... | custom-call | tf_op jit(solution)/shard_map/outer/pallas_call | solution.py:485
Async XLA Ops:
  2.7 40.6 %collective-permute-start.1 = (f32[560,128]{1,0:T(8,128)S(1)}, f32[560,128]{1,0:T(8,128)S(1)}, u32[]{:S(2)}, u32[]{:S(2)}) collective-permute-start(f32[560,128]{1,0:T(8,128)S(1)} %get-tuple-element.39), channel_id=1, source_target_pairs={{1,2},{2,1},{3,4},{4,3},{5,6},{6,5},{7,8},{8,7},{9,10},{10,9},{11,... | collective-permute-start | bytes 860168 | tf_op jit(solution)/shard_map/ppermute | solution.py:457
  20.1 23.1 %collective-permute-start = (f32[560,128]{1,0:T(8,128)S(1)}, f32[560,128]{1,0:T(8,128)S(1)}, u32[]{:S(2)}, u32[]{:S(2)}) collective-permute-start(f32[560,128]{1,0:T(8,128)S(1)} %get-tuple-element.38.refs_7_), channel_id=1, source_target_pairs={{0,1},{1,0},{2,3},{3,2},{4,5},{5,4},{6,7},{7,6},{8,9},{9,8},{10,11... | collective-permute-start | bytes 860168 | tf_op jit(solution)/shard_map/ppermute | solution.py:458
  44.1 9.3 %collective-permute-start.3 = (f32[400,128]{1,0:T(8,128)S(1)}, f32[400,128]{1,0:T(8,128)S(1)}, u32[]{:S(2)}, u32[]{:S(2)}) collective-permute-start(f32[400,128]{1,0:T(8,128)S(1)} %get-tuple-element.60), channel_id=1, source_target_pairs={{32,64},{64,32},{96,128},{128,96},{160,192},{192,160},{224,256},{2... | collective-permute-start | bytes 614408 | tf_op jit(solution)/shard_map/ppermute | solution.py:472
  46.1 7.3 %collective-permute-start.2 = (f32[400,128]{1,0:T(8,128)S(1)}, f32[400,128]{1,0:T(8,128)S(1)}, u32[]{:S(2)}, u32[]{:S(2)}) collective-permute-start(f32[400,128]{1,0:T(8,128)S(1)} %get-tuple-element.48.refs_6_), channel_id=1, source_target_pairs={{0,32},{32,0},{64,96},{96,64},{128,160},{160,128},{192,224},{224,1... | collective-permute-start | bytes 614408 | tf_op jit(solution)/shard_map/ppermute | solution.py:471
